TPU v7x, 256 devices: a whole 4x4x8 slice. The times are simulated.
256 devices in a mesh: row: 8 (over y, core), col: 16 (over z, x_hi), layer: 2 (over x_lo).
Axes of the slice: x: 4 (x_hi: 2, x_lo: 2; x = x_hi * 2 + x_lo), y: 4, z: 8, core: 2. Of those that a mesh axis runs over, the one named last changes fastest.
Arguments:
- a_tiles: float32 [128, 2, 7, 128, 128], P(('row', 'col'), 'layer'), may hold values from -0.5 to 0.5
- a_cols: int32 [128, 2, 7], P(('row', 'col'), 'layer'), may hold values from -1 to 255, as said below
- b_tiles: float32 [256, 2, 7, 128, 128], P(('row', 'col'), 'layer'), may hold values from -6 to 6
- b_rows: int32 [256, 2, 7], P(('row', 'col'), 'layer'), may hold values from 0 to 255, as said below
- c_cols: int32 [128, 16, 4], P('row', 'col'), may hold values from 0 to 255, as said below
Outputs:
- c_tiles: float32 [128, 16, 4, 128, 128], P('row', 'col', 'layer')
Inputs may be any that keep to these rules, and one draw needn't show every extreme that they name: In a_cols[i, h, :] the used slots come first and hold distinct block columns in [h * 128, (h + 1) * 128); the unused ones hold -1. Some block rows use all 7 slots in each half, others few. b_rows[j, h, :] holds 7 distinct block rows in [h * 128, (h + 1) * 128). c_cols[i, g, :] holds 4 distinct block columns j with (j // 2) % 16 == g.
All inputs are finite; a program needn't handle non-finite values.
Results may differ from a plain program's by a relative error of at most 0.0003.
Values sent between devices are 32-bit elements; how exact they have to be, the bound alone decides.
A program may use at most 128 MiB of HBM per device.

v0:
```python
import jax
import jax.numpy as jnp
from jax import lax
from jax.sharding import PartitionSpec as P


def split_up(value, dim, devices):
    dims = value.shape
    tiles = value.reshape(*dims[:dim], devices, dims[dim] // devices, *dims[dim + 1 :])
    return jnp.moveaxis(tiles, dim, 0)


def sent_and_summed(value, axis, dim):
    tiles = split_up(value, dim, lax.axis_size(axis))
    arrived = lax.all_to_all(tiles, axis, split_axis=0, concat_axis=0, tiled=True)
    return arrived.sum(axis=0)


def row_block(a_row, a_index, wanted, b_flat, b_index, block_width, group_count):
    halves = b_index.shape[1]
    slot_count = b_index.shape[2]
    panel_col = wanted // block_width // group_count * block_width + wanted % block_width
    col_rows = b_index[panel_col]
    matches = (col_rows[:, :, None, :] == a_index[None, :, :, None]) & (a_index >= 0)[
        None, :, :, None
    ]
    present = jnp.any(matches, axis=3)
    position = jnp.argmax(matches, axis=3)
    layer_ids = jnp.arange(halves, dtype=jnp.int32)
    flat_index = (
        panel_col[:, None, None] * halves + layer_ids[None, :, None]
    ) * slot_count + position
    chosen = jnp.take(b_flat, flat_index.reshape(-1), axis=0)
    chosen = chosen.reshape(flat_index.shape + b_flat.shape[1:])
    chosen = jnp.where(present[..., None, None], chosen, jnp.zeros((), chosen.dtype))
    return jnp.einsum("heab,qhebc->qac", a_row, chosen, precision=lax.Precision.HIGHEST)


def on_device(a_tiles, a_cols, b_tiles, b_rows, c_cols):
    block_width = b_tiles.shape[0]
    group_count = lax.axis_size("col")
    wanted = c_cols[:, 0, :]
    b_panel, b_index = (
        lax.all_gather(b_tiles, "row", axis=0, tiled=True),
        lax.all_gather(b_rows, "row", axis=0, tiled=True),
    )
    b_flat = b_panel.reshape((-1,) + b_panel.shape[3:])
    a_piece = lax.all_gather(a_tiles, "col", axis=0, tiled=True)
    index_piece = lax.all_gather(a_cols, "col", axis=0, tiled=True)

    def one_row(inputs):
        return row_block(inputs[0], inputs[1], inputs[2], b_flat, b_index, block_width, group_count)

    row_out = lax.map(one_row, (a_piece, index_piece, wanted))
    return sent_and_summed(row_out[:, None], "layer", 2)


def solution(mesh):
    return jax.shard_map(
        on_device,
        mesh=mesh,
        in_specs=(
            P(("row", "col"), "layer", None, None, None),
            P(("row", "col"), "layer", None),
            P(("row", "col"), "layer", None, None, None),
            P(("row", "col"), "layer", None),
            P("row", "col", None),
        ),
        out_specs=P("row", "col", "layer", None, None),
        check_vma=False,
    )
```

profile of v0, /device:TPU:1, one launch (start us, length us, event | category | flops | bytes accessed | tf_op | source)
XLA Modules:
  0.0 463.2 jit_solution(5467644045152591261)
XLA Ops:
  8.0 12.4 %all_gather.12 = s32[16,1,7]{2,1,0:T(1,128)S(1)} all-gather(s32[2,1,7]{2,1,0:T(1,128)} %param.10), channel_id=1, replica_groups=mesh['row'=8,'col'=16,'layer'=2] {'row'}, dimensions={0}, use_global_device_ids=true | all-gather | bytes 504 | tf_op jit(solution)/shard_map/all_gather | solution.py:45
  21.2 36.6 %all_gather.13 = s32[16,1,7]{2,1,0:T(1,128)S(1)} all-gather(s32[1,1,7]{2,1,0:T(1,128)} %param.8), channel_id=1, replica_groups=mesh['row'=8,'col'=16,'layer'=2] {'col'}, dimensions={0}, use_global_device_ids=true | all-gather | bytes 476 | tf_op jit(solution)/shard_map/all_gather | solution.py:49
  57.8 3.6 all-gather.3.cloned.1.call-done
  61.3 127.5 %all-gather.5.cloned.1.call-done = f32[16,1,7,128,128]{4,3,2,1,0:T(8,128)} async-done(((f32[1,1,7,128,128]{4,3,2,1,0:T(8,128)}), f32[16,1,7,128,128]{4,3,2,1,0:T(8,128)}) %all-gather.5.cloned.1.call-update) | async-done | bytes 7340048 | tf_op jit(solution)/shard_map/all_gather | solution.py:48
  188.8 203.9 %while.13 = (s32[]{:T(128)}, f32[16,4,128,128]{3,2,1,0:T(8,128)}, s32[16,4]{1,0:T(8,128)S(1)}, s32[16,1,7]{0,2,1:T(8,128)S(1)}, s32[16,1,7]{2,1,0:T(1,128)S(1)},...) while((s32[]{:T(128)}, f32[16,4,128,128]{3,2,1,0:T(8,128)}, ...), condition=%wide.region_3.4_spmd, body=%wide.region_0.3_spmd.sunk | while | flops 705565312 | bytes 10956954 | solution.py:54
  189.5 1.0 iota_reduce_fusion.2
  190.7 5.0 %gather_fusion.1 = f32[28,128,128]{2,1,0:T(8,128)} fusion(f32[112,128,128]{2,1,0:T(8,128)} %get-tuple-element.242, s32[1024]{0:T(1024)S(1)} %pad_clamp_fusion.5), kind=kCustom, calls=%fused_computation.1.clone.1 | custom fusion | bytes 3670128 | tf_op jit(solution)/shard_map/while/body/eval_jaxpr/jit(_take)/gather | solution.py:33
  195.7 1.8 copy.50
  197.9 2.8 fusion.36
  202.2 1.0 iota_reduce_fusion.2
  203.4 5.0 %gather_fusion.1 = f32[28,128,128]{2,1,0:T(8,128)} fusion(f32[112,128,128]{2,1,0:T(8,128)} %get-tuple-element.242, s32[1024]{0:T(1024)S(1)} %pad_clamp_fusion.5), kind=kCustom, calls=%fused_computation.1.clone.1 | custom fusion | bytes 3670128 | tf_op jit(solution)/shard_map/while/body/eval_jaxpr/jit(_take)/gather | solution.py:33
  208.4 1.8 copy.50
  210.6 2.8 fusion.36
  215.0 1.0 iota_reduce_fusion.2
  216.2 5.0 %gather_fusion.1 = f32[28,128,128]{2,1,0:T(8,128)} fusion(f32[112,128,128]{2,1,0:T(8,128)} %get-tuple-element.242, s32[1024]{0:T(1024)S(1)} %pad_clamp_fusion.5), kind=kCustom, calls=%fused_computation.1.clone.1 | custom fusion | bytes 3670128 | tf_op jit(solution)/shard_map/while/body/eval_jaxpr/jit(_take)/gather | solution.py:33
  221.2 1.8 copy.50
  223.4 2.8 fusion.36
  227.7 1.0 iota_reduce_fusion.2
  228.9 5.0 %gather_fusion.1 = f32[28,128,128]{2,1,0:T(8,128)} fusion(f32[112,128,128]{2,1,0:T(8,128)} %get-tuple-element.242, s32[1024]{0:T(1024)S(1)} %pad_clamp_fusion.5), kind=kCustom, calls=%fused_computation.1.clone.1 | custom fusion | bytes 3670128 | tf_op jit(solution)/shard_map/while/body/eval_jaxpr/jit(_take)/gather | solution.py:33
  233.9 1.8 copy.50
  236.1 2.8 fusion.36
  240.5 1.0 iota_reduce_fusion.2
  241.7 5.0 %gather_fusion.1 = f32[28,128,128]{2,1,0:T(8,128)} fusion(f32[112,128,128]{2,1,0:T(8,128)} %get-tuple-element.242, s32[1024]{0:T(1024)S(1)} %pad_clamp_fusion.5), kind=kCustom, calls=%fused_computation.1.clone.1 | custom fusion | bytes 3670128 | tf_op jit(solution)/shard_map/while/body/eval_jaxpr/jit(_take)/gather | solution.py:33
  246.6 1.8 copy.50
  248.9 2.8 fusion.36
  253.2 1.0 iota_reduce_fusion.2
  254.4 5.0 %gather_fusion.1 = f32[28,128,128]{2,1,0:T(8,128)} fusion(f32[112,128,128]{2,1,0:T(8,128)} %get-tuple-element.242, s32[1024]{0:T(1024)S(1)} %pad_clamp_fusion.5), kind=kCustom, calls=%fused_computation.1.clone.1 | custom fusion | bytes 3670128 | tf_op jit(solution)/shard_map/while/body/eval_jaxpr/jit(_take)/gather | solution.py:33
  259.4 1.8 copy.50
  261.6 2.8 fusion.36
  266.0 1.0 iota_reduce_fusion.2
  267.2 5.0 %gather_fusion.1 = f32[28,128,128]{2,1,0:T(8,128)} fusion(f32[112,128,128]{2,1,0:T(8,128)} %get-tuple-element.242, s32[1024]{0:T(1024)S(1)} %pad_clamp_fusion.5), kind=kCustom, calls=%fused_computation.1.clone.1 | custom fusion | bytes 3670128 | tf_op jit(solution)/shard_map/while/body/eval_jaxpr/jit(_take)/gather | solution.py:33
  272.1 1.8 copy.50
  274.4 2.8 fusion.36
  279.9 5.0 %gather_fusion.1 = f32[28,128,128]{2,1,0:T(8,128)} fusion(f32[112,128,128]{2,1,0:T(8,128)} %get-tuple-element.242, s32[1024]{0:T(1024)S(1)} %pad_clamp_fusion.5), kind=kCustom, calls=%fused_computation.1.clone.1 | custom fusion | bytes 3670128 | tf_op jit(solution)/shard_map/while/body/eval_jaxpr/jit(_take)/gather | solution.py:33
  284.9 1.8 copy.50
  287.1 2.8 fusion.36
  292.6 5.0 %gather_fusion.1 = f32[28,128,128]{2,1,0:T(8,128)} fusion(f32[112,128,128]{2,1,0:T(8,128)} %get-tuple-element.242, s32[1024]{0:T(1024)S(1)} %pad_clamp_fusion.5), kind=kCustom, calls=%fused_computation.1.clone.1 | custom fusion | bytes 3670128 | tf_op jit(solution)/shard_map/while/body/eval_jaxpr/jit(_take)/gather | solution.py:33
  297.6 1.8 copy.50
  299.8 2.8 fusion.36
  305.4 5.0 %gather_fusion.1 = f32[28,128,128]{2,1,0:T(8,128)} fusion(f32[112,128,128]{2,1,0:T(8,128)} %get-tuple-element.242, s32[1024]{0:T(1024)S(1)} %pad_clamp_fusion.5), kind=kCustom, calls=%fused_computation.1.clone.1 | custom fusion | bytes 3670128 | tf_op jit(solution)/shard_map/while/body/eval_jaxpr/jit(_take)/gather | solution.py:33
  310.3 1.8 copy.50
  312.6 2.8 fusion.36
  318.1 5.0 %gather_fusion.1 = f32[28,128,128]{2,1,0:T(8,128)} fusion(f32[112,128,128]{2,1,0:T(8,128)} %get-tuple-element.242, s32[1024]{0:T(1024)S(1)} %pad_clamp_fusion.5), kind=kCustom, calls=%fused_computation.1.clone.1 | custom fusion | bytes 3670128 | tf_op jit(solution)/shard_map/while/body/eval_jaxpr/jit(_take)/gather | solution.py:33
  323.1 1.8 copy.50
  325.3 2.8 fusion.36
  330.8 5.0 %gather_fusion.1 = f32[28,128,128]{2,1,0:T(8,128)} fusion(f32[112,128,128]{2,1,0:T(8,128)} %get-tuple-element.242, s32[1024]{0:T(1024)S(1)} %pad_clamp_fusion.5), kind=kCustom, calls=%fused_computation.1.clone.1 | custom fusion | bytes 3670128 | tf_op jit(solution)/shard_map/while/body/eval_jaxpr/jit(_take)/gather | solution.py:33
  335.8 1.8 copy.50
  338.0 2.8 fusion.36
  343.6 5.0 %gather_fusion.1 = f32[28,128,128]{2,1,0:T(8,128)} fusion(f32[112,128,128]{2,1,0:T(8,128)} %get-tuple-element.242, s32[1024]{0:T(1024)S(1)} %pad_clamp_fusion.5), kind=kCustom, calls=%fused_computation.1.clone.1 | custom fusion | bytes 3670128 | tf_op jit(solution)/shard_map/while/body/eval_jaxpr/jit(_take)/gather | solution.py:33
  348.6 1.8 copy.50
  350.8 2.8 fusion.36
  356.3 5.0 %gather_fusion.1 = f32[28,128,128]{2,1,0:T(8,128)} fusion(f32[112,128,128]{2,1,0:T(8,128)} %get-tuple-element.242, s32[1024]{0:T(1024)S(1)} %pad_clamp_fusion.5), kind=kCustom, calls=%fused_computation.1.clone.1 | custom fusion | bytes 3670128 | tf_op jit(solution)/shard_map/while/body/eval_jaxpr/jit(_take)/gather | solution.py:33
  361.3 1.8 copy.50
  363.5 2.8 fusion.36
  369.1 5.0 %gather_fusion.1 = f32[28,128,128]{2,1,0:T(8,128)} fusion(f32[112,128,128]{2,1,0:T(8,128)} %get-tuple-element.242, s32[1024]{0:T(1024)S(1)} %pad_clamp_fusion.5), kind=kCustom, calls=%fused_computation.1.clone.1 | custom fusion | bytes 3670128 | tf_op jit(solution)/shard_map/while/body/eval_jaxpr/jit(_take)/gather | solution.py:33
  374.1 1.8 copy.50
  376.3 2.8 fusion.36
  381.9 5.0 %gather_fusion.1 = f32[28,128,128]{2,1,0:T(8,128)} fusion(f32[112,128,128]{2,1,0:T(8,128)} %get-tuple-element.242, s32[1024]{0:T(1024)S(1)} %pad_clamp_fusion.5), kind=kCustom, calls=%fused_computation.1.clone.1 | custom fusion | bytes 3670128 | tf_op jit(solution)/shard_map/while/body/eval_jaxpr/jit(_take)/gather | solution.py:33
  386.8 1.8 copy.50
  389.1 2.8 fusion.36
  392.7 5.4 %copy.35 = f32[2,16,1,2,128,128]{4,5,3,1,2,0:T(8,128)} copy(f32[2,16,1,2,128,128]{5,4,3,0,1,2:T(8,128)} %bitcast.84) | data formatting | bytes 8388608 | tf_op jit(solution)/shard_map/transpose | solution.py:10
  398.1 53.7 %all_to_all.5 = f32[2,16,1,2,128,128]{4,5,3,1,2,0:T(8,128)} all-to-all(f32[2,16,1,2,128,128]{4,5,3,1,2,0:T(8,128)} %copy.35), channel_id=1, replica_groups=mesh['row'=8,'col'=16,'layer'=2] {'layer'}, dimensions={0} | all-to-all | bytes 8388608 | tf_op jit(solution)/shard_map/all_to_all | solution.py:15
  451.8 2.7 reduce_sum.11
  454.5 1.8 copy.37
  (272 shorter events, 45.8 us)
Async XLA Ops:
  6.5 54.8 %all-gather.3.cloned.1.call-start = ((), (), s32[]{:S(2)}) async-start(), calls=%async_computation.1 | async-start | bytes 8257536 | tf_op jit(solution)/shard_map/all_gather | solution.py:44
  7.3 181.5 %all-gather.5.cloned.1.call-start = ((), (), s32[]{:S(2)}) async-start(), calls=%async_computation.2 | async-start | bytes 7798784 | tf_op jit(solution)/shard_map/all_gather | solution.py:48
Sparse Core Ops, SparseCore 0:
  9.2 52.1 all-gather.2
  63.9 124.8 all-gather.4
where the time goes:
time: 466 us; the launch traced here: 463 us
  local copies, waits for them, and re-layouts  145 us (31%)
  waiting for transfers between devices  132 us (28%)
  blocking collectives  103 us (22%)
  matrix products  44.3 us (10%)
  other arithmetic  24.2 us (5%)
  between operations  13.4 us (3%)
    all_gather x1, waiting for transfers between devices, on_device(): a_piece = lax.all_gather(a_tiles, 'col', axis=0, tiled=True)  127 us
    gather x32, local copies, waits for them, and re-layouts, row_block(): chosen = jnp.take(b_flat, flat_index.reshape(-1), axis=0)  109 us
    all_to_all x1, blocking collectives, sent_and_summed(): lax.all_to_all(tiles, axis, split_axis=0, concat_axis=0, tiled=True)  53.7 us
    dot_general x16, matrix products, row_block(): jnp.einsum('heab,qhebc->qac', a_row, chosen, precision=lax.Precision.HIGH...  44.3 us
    all_gather x1, blocking collectives, on_device(): index_piece = lax.all_gather(a_cols, 'col', axis=0, tiled=True)  36.6 us
    another operation x16, other arithmetic, row_block(): position = jnp.argmax(matches, axis=3)  15.4 us
    dynamic_update_slice x32, local copies, waits for them, and re-layouts, on_device(): row_out = lax.map(one_row, (a_piece, index_piece, wanted))  13.8 us
    all_gather x1, blocking collectives, on_device(): lax.all_gather(b_rows, 'row', axis=0, tiled=True)  12.4 us
  transfers between devices with their start and end apart: 2, of which 2 were waited for; matrix products, arithmetic and copies ran while one was open for 0% of the time, Pallas kernels for 0%

commit v1 on v0

v1 whole, which is shorter than its diff:
```python
import jax
import jax.numpy as jnp
from jax import lax
from jax.experimental import pallas as pl
from jax.experimental.pallas import tpu as pltpu
from jax.sharding import PartitionSpec as P

MESH = pl.DeviceIdType.MESH
TILE = 128
SLOTS = 7
A_ROWS = SLOTS * TILE
B_TILES = 2 * SLOTS
B_ROWS = B_TILES * TILE
N_ROW, N_COL = 8, 16
B_ALL = N_ROW * B_TILES
HALF_A = A_ROWS // 2
HALF_B = B_ROWS // 2


def source_col(k, z, x_hi):
    distance = (k + 2) // 4
    other = (k // 2 + 1 + (15 - k) // 15 + k // 15) % 2
    sign = 2 * (k % 2) - 1
    return ((z + sign * distance + 8) % 8) * 2 + (x_hi + other) % 2


def kernel(
    want_ref,
    a_index_ref,
    b_index_ref,
    a_ref,
    b_ref,
    out_ref,
    a_all,
    b_all,
    b_hi,
    b_lo,
    a_index_all,
    b_index_all,
    table_vmem,
    table,
    lhs,
    rhs,
    to_send,
    own_part,
    arrived,
    local_sem,
    ai_send,
    ai_recv,
    bi_send,
    bi_recv,
    a_send,
    a_recv,
    b_send,
    b_recv,
    c_send,
    c_recv,
    out_sem,
):
    row, col, layer = lax.axis_index("row"), lax.axis_index("col"), lax.axis_index("layer")
    z, x_hi = col // 2, col % 2
    y, core = row // 2, row % 2

    def at(r, c, l):
        return (r, c, l)

    z_up = at(row, (col + 2) % N_COL, layer)
    z_down = at(row, (col + N_COL - 2) % N_COL, layer)
    x_far = at(row, z * 2 + (x_hi + 1) % 2, layer)
    y_up_row, y_down_row, y_far_row = (row + 2) % N_ROW, (row + 6) % N_ROW, (row + 4) % N_ROW
    y_up, y_down = at(y_up_row, col, layer), at(y_down_row, col, layer)
    sibling_row = y * 2 + (core + 1) % 2
    sibling = at(sibling_row, col, layer)
    sib_up, sib_down, sib_far = (
        (sibling_row + 2) % N_ROW,
        (sibling_row + 6) % N_ROW,
        (sibling_row + 4) % N_ROW,
    )
    partner = at(row, col, 1 - layer)

    def remote(src, dst, send_sem, recv_sem, device):
        return pltpu.make_async_remote_copy(
            src_ref=src,
            dst_ref=dst,
            send_sem=send_sem,
            recv_sem=recv_sem,
            device_id=device,
            device_id_type=MESH,
        )

    barrier = pltpu.get_barrier_semaphore()

    @pl.loop(1, N_COL)
    def _(d):
        pl.semaphore_signal(
            barrier, inc=1, device_id=at(row, (col + d) % N_COL, layer), device_id_type=MESH
        )

    @pl.loop(1, N_ROW)
    def _(d):
        pl.semaphore_signal(
            barrier, inc=1, device_id=at((row + d) % N_ROW, col, layer), device_id_type=MESH
        )

    pl.semaphore_signal(barrier, inc=1, device_id=partner, device_id_type=MESH)
    pl.semaphore_wait(barrier, N_COL + N_ROW - 1)

    def a_index_copy(d):
        return remote(
            a_index_ref,
            a_index_all.at[col],
            ai_send.at[d],
            ai_recv.at[d],
            at(row, (col + d) % N_COL, layer),
        )

    def b_index_copy(d):
        return remote(
            b_index_ref,
            b_index_all.at[row],
            bi_send.at[d],
            bi_recv.at[d],
            at((row + d) % N_ROW, col, layer),
        )

    @pl.loop(1, N_ROW)
    def _(d):
        b_index_copy(d).start()

    @pl.loop(1, N_COL)
    def _(d):
        a_index_copy(d).start()

    first, second = pl.ds(0, HALF_B), pl.ds(HALF_B, HALF_B)
    b_own_up = remote(b_ref, b_all.at[row], b_send.at[0], b_recv.at[0], y_up)
    b_own_down = remote(b_ref, b_all.at[row], b_send.at[1], b_recv.at[1], y_down)
    b_own_sib = remote(b_ref, b_all.at[row], b_send.at[2], b_recv.at[4], sibling)
    b_fwd_up = remote(
        b_all.at[y_down_row, first], b_all.at[y_down_row, first], b_send.at[3], b_recv.at[2], y_up
    )
    b_fwd_down = remote(
        b_all.at[y_up_row, second], b_all.at[y_up_row, second], b_send.at[4], b_recv.at[3], y_down
    )
    b_down_sib = remote(
        b_all.at[y_down_row], b_all.at[y_down_row], b_send.at[5], b_recv.at[5], sibling
    )
    b_up_sib = remote(b_all.at[y_up_row], b_all.at[y_up_row], b_send.at[6], b_recv.at[6], sibling)
    b_far_sib = [
        remote(
            b_all.at[y_far_row, part],
            b_all.at[y_far_row, part],
            b_send.at[7 + n],
            b_recv.at[7 + n],
            sibling,
        )
        for n, part in enumerate((first, second))
    ]
    b_own_up.start()
    b_own_down.start()

    a_far = remote(a_ref, a_all.at[1], a_send.at[16], a_recv.at[1], x_far)
    a_up = remote(a_ref, a_all.at[2], a_send.at[14], a_recv.at[2], z_up)
    a_down = remote(a_ref, a_all.at[3], a_send.at[15], a_recv.at[3], z_down)
    a_far.start()
    a_up.start()
    a_down.start()
    b_own_sib.start()
    a_local = pltpu.make_async_copy(a_ref, a_all.at[0], local_sem.at[0])
    b_local = pltpu.make_async_copy(b_ref, b_all.at[row], local_sem.at[1])
    a_local.start()
    b_local.start()

    a_index_all[col] = a_index_ref[...]
    b_index_all[row] = b_index_ref[...]
    b_hi[B_ALL] = jnp.zeros((TILE, TILE), jnp.bfloat16)
    b_lo[B_ALL] = jnp.zeros((TILE, TILE), jnp.bfloat16)

    @pl.loop(1, N_ROW)
    def _(d):
        b_index_copy(d).wait()

    @pl.loop(1, N_COL)
    def _(d):
        a_index_copy(d).wait()

    b_index = b_index_all[0]
    for r in range(1, N_ROW):
        b_index = jnp.maximum(b_index, b_index_all[r])
    lane = lax.broadcasted_iota(jnp.int32, (8, TILE), 1)
    panel = lane // SLOTS

    def one_row(i, found):
        a_index = a_index_all[i]
        for q in range(4):
            wanted = want_ref[i, q]
            wanted_panel = wanted // 32 * 2 + wanted % 2
            match = (a_index == b_index) & (panel == wanted_panel)
            position = jnp.min(jnp.where(match, lane, B_ALL), axis=1, keepdims=True)
            found = jnp.where(lane == i * 4 + q, position, found)
        return found

    table_vmem[...] = lax.fori_loop(0, N_COL, one_row, jnp.full((8, TILE), B_ALL, jnp.int32))
    to_table = pltpu.make_async_copy(table_vmem, table, local_sem.at[2])
    to_table.start()
    to_table.wait()

    def split_b(r):
        @pl.loop(0, B_TILES)
        def _(t):
            value = b_all[r, pl.ds(pl.multiple_of(t * TILE, TILE), TILE), :]
            hi = value.astype(jnp.bfloat16)
            b_hi[r * B_TILES + t] = hi
            b_lo[r * B_TILES + t] = (value - hi.astype(jnp.float32)).astype(jnp.bfloat16)

    def a_forward(k):
        ahead = (col + (1 - k % 2) * 2 + (k % 2) * (N_COL - 2)) % N_COL
        return remote(
            a_all.at[k], a_all.at[k + 4], a_send.at[k], a_recv.at[k + 4], at(row, ahead, layer)
        )

    def a_forward_half(k):
        ahead = (col + (1 - k % 2) * 2 + (k % 2) * (N_COL - 2)) % N_COL
        part = pl.ds(pl.multiple_of((k % 2) * HALF_A, HALF_A), HALF_A)
        return remote(
            a_all.at[k, part],
            a_all.at[14 + (k - 10) // 2, part],
            a_send.at[k],
            a_recv.at[k + 4],
            at(row, ahead, layer),
        )

    a_far_up = remote(a_all.at[1], a_all.at[4], a_send.at[0], a_recv.at[4], z_up)
    a_far_down = remote(a_all.at[1], a_all.at[5], a_send.at[1], a_recv.at[5], z_down)

    def a_arrival(k):
        return remote(a_all.at[k], a_all.at[k], a_send.at[k], a_recv.at[k], z_up)

    def a_arrival_half(k, n):
        part = pl.ds(n * HALF_A, HALF_A)
        return remote(
            a_all.at[k, part],
            a_all.at[k, part],
            a_send.at[k],
            a_recv.at[14 + 2 * (k - 14) + n],
            z_up,
        )

    b_local.wait()
    split_b(row)
    for k in (2, 3):
        a_arrival(k).wait_recv()
        a_forward(k).start()
    b_own_sib.wait_recv()
    split_b(sibling_row)
    a_arrival(1).wait_recv()
    a_far_up.start()
    a_far_down.start()
    b_own_up.wait_recv()
    b_fwd_up.start()
    b_down_sib.start()
    b_own_down.wait_recv()
    b_fwd_down.start()
    b_up_sib.start()
    split_b(y_down_row)
    split_b(y_up_row)
    b_down_sib.wait_recv()
    split_b(sib_down)
    b_up_sib.wait_recv()
    split_b(sib_up)
    for k in (6, 7):
        a_arrival(k).wait_recv()
        a_forward(k).start()
    b_fwd_up.wait_recv()
    b_far_sib[0].start()
    b_fwd_down.wait_recv()
    b_far_sib[1].start()
    split_b(y_far_row)
    for k in (4, 5):
        a_arrival(k).wait_recv()
        a_forward(k).start()
    b_far_sib[0].wait_recv()
    b_far_sib[1].wait_recv()
    split_b(sib_far)
    a_local.wait()

    def c_copy(k):
        return remote(to_send.at[k], arrived.at[k], c_send.at[k], c_recv.at[k], partner)

    def out_copy(k):
        return pltpu.make_async_copy(
            own_part.at[k], out_ref.at[source_col(k, z, x_hi)], out_sem.at[k]
        )

    def terms(i, half):
        for s in range(SLOTS):
            for n in range(2):
                t = table[s, i * 4 + half * 2 + n]
                rhs[0, s * TILE : (s + 1) * TILE, n * TILE : (n + 1) * TILE] = b_hi[t]
                rhs[1, s * TILE : (s + 1) * TILE, n * TILE : (n + 1) * TILE] = b_lo[t]
        both = jnp.dot(lhs[...], rhs[0], preferred_element_type=jnp.float32)
        low = jnp.dot(lhs[0:TILE, :], rhs[1], preferred_element_type=jnp.float32)
        return both[0:TILE] + (both[TILE : 2 * TILE] + low)

    def finish(k):
        c_copy(k).wait_recv()
        own_part[k] = own_part[k] + arrived[k]
        out_copy(k).start()

    @pl.loop(0, 16)
    def _(k):
        @pl.when((k >= 8) & (k < 14))
        def _():
            a_arrival(k).wait_recv()

        @pl.when((k >= 8) & (k < 10))
        def _():
            a_forward(k).start()

        @pl.when((k >= 10) & (k < 14))
        def _():
            a_forward_half(k).start()

        @pl.when(k >= 14)
        def _():
            a_arrival_half(k, 0).wait_recv()
            a_arrival_half(k, 1).wait_recv()

        i = source_col(k, z, x_hi)
        for s in range(SLOTS):
            value = a_all[k, s * TILE : (s + 1) * TILE, :]
            hi = value.astype(jnp.bfloat16)
            lhs[0:TILE, s * TILE : (s + 1) * TILE] = hi
            lhs[TILE : 2 * TILE, s * TILE : (s + 1) * TILE] = (
                value - hi.astype(jnp.float32)
            ).astype(jnp.bfloat16)
        theirs = terms(i, 1 - layer)
        to_send[k, 0] = theirs[:, 0:TILE]
        to_send[k, 1] = theirs[:, TILE : 2 * TILE]
        c_copy(k).start()
        ours = terms(i, layer)
        own_part[k, 0] = ours[:, 0:TILE]
        own_part[k, 1] = ours[:, TILE : 2 * TILE]

        @pl.when(k >= 8)
        def _():
            finish(k - 8)

    @pl.loop(8, 16)
    def _(k):
        finish(k)

    @pl.loop(0, 16)
    def _(k):
        out_copy(k).wait()
        c_copy(k).wait_send()

    for copy in (a_far, a_up, a_down, a_far_up, a_far_down):
        copy.wait_send()

    @pl.loop(2, 10)
    def _(k):
        a_forward(k).wait_send()

    @pl.loop(10, 14)
    def _(k):
        a_forward_half(k).wait_send()

    for copy in (b_own_up, b_own_down, b_own_sib, b_fwd_up, b_fwd_down, b_down_sib, b_up_sib):
        copy.wait_send()
    for copy in b_far_sib:
        copy.wait_send()


def on_device(a_tiles, a_cols, b_tiles, b_rows, c_cols):
    row = lax.axis_index("row")
    a_index = jnp.broadcast_to(
        jnp.pad(a_cols.reshape(SLOTS, 1), ((0, 1), (0, 0)), constant_values=-1), (8, TILE)
    )
    b_index = lax.dynamic_update_slice(
        jnp.full((8, TILE), -5, jnp.int32),
        jnp.broadcast_to(b_rows.reshape(1, B_TILES), (8, B_TILES)),
        (0, row * B_TILES),
    )
    f32, i32, bf16 = jnp.float32, jnp.int32, jnp.bfloat16
    dma = pltpu.SemaphoreType.DMA
    anywhere = pl.BlockSpec(memory_space=pl.ANY)
    in_vmem = pl.BlockSpec(memory_space=pltpu.VMEM)
    out = pl.pallas_call(
        kernel,
        out_shape=jax.ShapeDtypeStruct((16, 2, TILE, TILE), f32),
        in_specs=[pl.BlockSpec(memory_space=pltpu.SMEM), in_vmem, in_vmem, anywhere, anywhere],
        out_specs=anywhere,
        scratch_shapes=[
            pltpu.VMEM((16, A_ROWS, TILE), f32),
            pltpu.VMEM((N_ROW, B_ROWS, TILE), f32),
            pltpu.VMEM((B_ALL + 1, TILE, TILE), bf16),
            pltpu.VMEM((B_ALL + 1, TILE, TILE), bf16),
            pltpu.VMEM((N_COL, 8, TILE), i32),
            pltpu.VMEM((N_ROW, 8, TILE), i32),
            pltpu.VMEM((8, TILE), i32),
            pltpu.SMEM((8, TILE), i32),
            pltpu.VMEM((2 * TILE, A_ROWS), bf16),
            pltpu.VMEM((2, A_ROWS, 2 * TILE), bf16),
            pltpu.VMEM((16, 2, TILE, TILE), f32),
            pltpu.VMEM((16, 2, TILE, TILE), f32),
            pltpu.VMEM((16, 2, TILE, TILE), f32),
            dma((3,)),
            dma((N_COL,)),
            dma((N_COL,)),
            dma((N_ROW,)),
            dma((N_ROW,)),
            dma((17,)),
            dma((18,)),
            dma((9,)),
            dma((9,)),
            dma((16,)),
            dma((16,)),
            dma((16,)),
        ],
        compiler_params=pltpu.CompilerParams(
            collective_id=0, has_side_effects=True, vmem_limit_bytes=48 * 2**20
        ),
        cost_estimate=pl.CostEstimate(
            flops=6 * 16 * 28 * TILE**3, bytes_accessed=4 * 2**20, transcendentals=0
        ),
        name="gather_multiply_sum",
    )(
        c_cols[:, 0, :],
        a_index,
        b_index,
        a_tiles.reshape(A_ROWS, TILE),
        b_tiles.reshape(B_ROWS, TILE),
    )
    return out[:, None]


def solution(mesh):
    return jax.shard_map(
        on_device,
        mesh=mesh,
        in_specs=(
            P(("row", "col"), "layer", None, None, None),
            P(("row", "col"), "layer", None),
            P(("row", "col"), "layer", None, None, None),
            P(("row", "col"), "layer", None),
            P("row", "col", None),
        ),
        out_specs=P("row", "col", "layer", None, None),
        check_vma=False,
    )
```

time: 466 us -> 103 us (0.22)
  local copies, waits for them, and re-layouts: 145 us -> 5.81 us
  waiting for transfers between devices: 132 us -> 0 us
  blocking collectives: 103 us -> 0 us
  Pallas kernels: 0 us -> 96 us
  matrix products: 44.3 us -> 0 us
  other arithmetic: 24.2 us -> 1.34 us
  between operations: 13.4 us -> 0.02 us
    all_gather x2 -> x0, waiting for transfers between devices: 131 us -> none  [the longest x1 127 us: on_device(): a_piece = lax.all_gather(a_tiles, 'col', axis=0, tiled=True)]
    gather x48 -> x0, local copies, waits for them, and re-layouts: 117 us -> none  [the longest x32 109 us: row_block(): chosen = jnp.take(b_flat, flat_index.reshape(-1), axis=0)]
    pallas_call x0 -> x1, Pallas kernels: none -> 96 us  [on_device(): pl.pallas_call(kernel, out_shape=jax.ShapeDtypeStruct((16, 2, TILE, TILE)...]
    all_to_all x1 -> x0, blocking collectives: 53.7 us -> none  [sent_and_summed(): lax.all_to_all(tiles, axis, split_axis=0, concat_axis=0, tiled=True)]
    all_gather x2 -> x0, blocking collectives: 48.9 us -> none  [the longest x1 36.6 us: on_device(): index_piece = lax.all_gather(a_cols, 'col', axis=0, tiled=True)]
    dot_general x16 -> x0, matrix products: 44.3 us -> none  [row_block(): jnp.einsum('heab,qhebc->qac', a_row, chosen, precision=lax.Precision.HIGH...]
    another operation x16 -> x0, other arithmetic: 15.4 us -> none  [row_block(): position = jnp.argmax(matches, axis=3)]
    dynamic_update_slice x32 -> x1, local copies, waits for them, and re-layouts: 13.8 us -> 0.2 us  [on_device(): lax.dynamic_update_slice(jnp.full((8, TILE), -5, jnp.int32), jnp.broadcas...]
  transfers between devices with their start and end apart: 2 -> 0, of which waited for: 2 -> 0; matrix products, arithmetic and copies ran while one was open for 0% -> 0% of each run, Pallas kernels for 0% -> 0%
where the time goes in v1:
time: 103 us
  Pallas kernels  96 us (93%)
  local copies, waits for them, and re-layouts  5.81 us (6%)
  other arithmetic  1.34 us (1%)
    pallas_call x1, Pallas kernels, on_device(): pl.pallas_call(kernel, out_shape=jax.ShapeDtypeStruct((16, 2, TILE, TILE)...  96 us
    unnamed x6, local copies, waits for them, and re-layouts  4.03 us

profile of v1, /device:TPU:1, one launch (start us, length us, event | category | flops | bytes accessed | tf_op | source)
XLA Modules:
  0.0 103.1 jit_solution(9945872479129971920)
XLA Ops:
  0.0 0.7 pad_bitcast_fusion
  0.7 0.5 broadcast.5
  1.2 1.3 %reduce.3 = s32[2,7]{1,0:T(2,128)S(1)} reduce(s32[2,1,7]{2,1,0:T(1,128)} %param.8, s32[]{:T(128)} %broadcast.5), dimensions={1}, to_apply=%param.8.reduce_sub_computation.3 | reduce | bytes 116 | tf_op args[3]
  2.5 0.1 broadcast_in_dim.23
  2.6 0.1 broadcast_in_dim.21.a_index_ref
  2.7 0.2 dynamic_update_slice.3.b_index_ref
  2.9 0.8 copy.6.want_ref
  3.6 0.0 copy-start
  3.6 1.2 %copy-done = f32[2,1,7,128,128]{4,3,2,1,0:T(8,128)S(1)} copy-done((f32[2,1,7,128,128]{4,3,2,1,0:T(8,128)S(1)}, f32[2,1,7,128,128]{4,3,2,1,0:T(8,128)}, u32[]{:S(2)}) %copy-start) | copy-done | bytes 917528
  4.8 0.0 copy-start.1
  4.8 1.0 copy-done.1
  5.8 96.0 %gather_multiply_sum.1 = f32[16,2,128,128]{3,2,1,0:T(8,128)S(1)} custom-call(s32[16,4]{1,0:T(8,128)S(1)} %copy.6.want_ref, s32[8,128]{1,0:T(8,128)S(1)} %broadcast_in_dim.21.a_index_ref, s32[8,128]{1,0:T(8,128)S(1)} %dynamic_update_slice.3.b_index_ref, f32[896,128]{1,0:T(8,128)S(1)} %bitcast.11, f32[1792,128]{1,0:T(8,128)S(1)} %bitcast.10), custom_call_target="tpu_custom_call" | custom-call | flops 5637144576 | bytes 4194304 | tf_op jit(solution)/shard_map/gather_multiply_sum/pallas_call | solution.py:388
  101.8 1.3 %copy.10 = f32[16,1,2,128,128]{4,3,2,1,0:T(8,128)} copy(f32[16,1,2,128,128]{4,3,2,1,0:T(8,128)S(1)} %bitcast.9) | data formatting | bytes 4194304
  (2 shorter events, 0.0 us)
Async XLA Ops:
  3.6 1.2 %copy-start = (f32[2,1,7,128,128]{4,3,2,1,0:T(8,128)S(1)}, f32[2,1,7,128,128]{4,3,2,1,0:T(8,128)}, u32[]{:S(2)}) copy-start(f32[2,1,7,128,128]{4,3,2,1,0:T(8,128)} %param.7) | copy-start | bytes 2752516
  4.8 1.0 copy-start.1

commit v2 on v1

v2 whole, which is shorter than its diff:
```python
import jax
import jax.numpy as jnp
from jax import lax
from jax.experimental import pallas as pl
from jax.experimental.pallas import tpu as pltpu
from jax.sharding import PartitionSpec as P

MESH = pl.DeviceIdType.MESH
TILE = 128
SLOTS = 7
A_ROWS = SLOTS * TILE
B_TILES = 2 * SLOTS
B_ROWS = B_TILES * TILE
N_ROW, N_COL = 8, 16
B_ALL = N_ROW * B_TILES
HALF_A = A_ROWS // 2


def source_col(k, z, x_hi):
    distance = (k + 2) // 4
    other = (k // 2 + 1 + (15 - k) // 15 + k // 15) % 2
    sign = 2 * (k % 2) - 1
    return ((z + sign * distance + 8) % 8) * 2 + (x_hi + other) % 2


def kernel(
    want_ref,
    a_cols_ref,
    b_rows_ref,
    a_ref,
    b_ref,
    own_ref,
    arrived_ref,
    a_all,
    b_all,
    b_hi,
    b_lo,
    want,
    a_cols,
    b_rows,
    a_index_all,
    b_index_all,
    a_index_own,
    b_index_own,
    table_vmem,
    table,
    lhs,
    rhs,
    to_send,
    local_sem,
    ai_send,
    ai_recv,
    bi_send,
    bi_recv,
    a_send,
    a_recv,
    b_send,
    b_recv,
    c_send,
    c_recv,
):
    row, col, layer = lax.axis_index("row"), lax.axis_index("col"), lax.axis_index("layer")
    z, x_hi = col // 2, col % 2
    y, core = row // 2, row % 2

    def at(r, c, l):
        return (r, c, l)

    z_up = at(row, (col + 2) % N_COL, layer)
    z_down = at(row, (col + N_COL - 2) % N_COL, layer)
    x_far = at(row, z * 2 + (x_hi + 1) % 2, layer)
    y_up_row, y_down_row, y_far_row = (row + 2) % N_ROW, (row + 6) % N_ROW, (row + 4) % N_ROW
    y_up, y_down = at(y_up_row, col, layer), at(y_down_row, col, layer)
    sibling_row = y * 2 + (core + 1) % 2
    sibling = at(sibling_row, col, layer)
    sib_up, sib_down, sib_far = (
        (sibling_row + 2) % N_ROW,
        (sibling_row + 6) % N_ROW,
        (sibling_row + 4) % N_ROW,
    )
    partner = at(row, col, 1 - layer)

    def remote(src, dst, send_sem, recv_sem, device):
        return pltpu.make_async_remote_copy(
            src_ref=src,
            dst_ref=dst,
            send_sem=send_sem,
            recv_sem=recv_sem,
            device_id=device,
            device_id_type=MESH,
        )

    a_local = pltpu.make_async_copy(a_ref, a_all.at[0], local_sem.at[0])
    b_local = pltpu.make_async_copy(b_ref, b_all.at[row], local_sem.at[1])
    scalars = [
        pltpu.make_async_copy(src, dst, local_sem.at[3 + n])
        for n, (src, dst) in enumerate(
            ((a_cols_ref, a_cols), (b_rows_ref, b_rows), (want_ref, want))
        )
    ]

    barrier = pltpu.get_barrier_semaphore()

    @pl.loop(1, N_COL)
    def _(d):
        pl.semaphore_signal(
            barrier, inc=1, device_id=at(row, (col + d) % N_COL, layer), device_id_type=MESH
        )

    @pl.loop(1, N_ROW)
    def _(d):
        pl.semaphore_signal(
            barrier, inc=1, device_id=at((row + d) % N_ROW, col, layer), device_id_type=MESH
        )

    pl.semaphore_signal(barrier, inc=1, device_id=partner, device_id_type=MESH)
    for copy in scalars:
        copy.start()
    b_local.start()
    a_local.start()
    for copy in scalars:
        copy.wait()
    lane = lax.broadcasted_iota(jnp.int32, (8, TILE), 1)
    sublane = lax.broadcasted_iota(jnp.int32, (8, TILE), 0)
    a_index = jnp.full((8, TILE), -1, jnp.int32)
    for s in range(SLOTS):
        a_index = jnp.where(sublane == s, a_cols[0, 0, s], a_index)
    b_index = jnp.full((8, TILE), -5, jnp.int32)
    for t in range(B_TILES):
        b_index = jnp.where(lane == row * B_TILES + t, b_rows[t // SLOTS, 0, t % SLOTS], b_index)
    a_index_own[...] = a_index
    b_index_own[...] = b_index
    a_index_all[col] = a_index
    b_index_all[row] = b_index
    b_hi[B_ALL] = jnp.zeros((TILE, TILE), jnp.bfloat16)
    b_lo[B_ALL] = jnp.zeros((TILE, TILE), jnp.bfloat16)
    pl.semaphore_wait(barrier, N_COL + N_ROW - 1)

    def a_index_copy(d):
        return remote(
            a_index_own,
            a_index_all.at[col],
            ai_send.at[d],
            ai_recv.at[d],
            at(row, (col + d) % N_COL, layer),
        )

    def b_index_copy(d):
        return remote(
            b_index_own,
            b_index_all.at[row],
            bi_send.at[d],
            bi_recv.at[d],
            at((row + d) % N_ROW, col, layer),
        )

    b_own_up = remote(b_ref, b_all.at[row], b_send.at[0], b_recv.at[0], y_up)
    b_own_down = remote(b_ref, b_all.at[row], b_send.at[1], b_recv.at[1], y_down)
    b_own_sib = remote(b_ref, b_all.at[row], b_send.at[2], b_recv.at[2], sibling)
    b_down_sib = remote(
        b_all.at[y_down_row], b_all.at[y_down_row], b_send.at[3], b_recv.at[3], sibling
    )
    b_up_sib = remote(b_all.at[y_up_row], b_all.at[y_up_row], b_send.at[4], b_recv.at[4], sibling)
    b_pieces = ((0, 4), (7, 4), (4, 3), (11, 3))
    b_forward, b_far_sib = [], []
    for n, (tile, count) in enumerate(b_pieces):
        part = pl.ds(tile * TILE, count * TILE)
        came, goes = (y_down_row, y_up) if n % 2 == 0 else (y_up_row, y_down)
        b_forward.append(
            remote(
                b_all.at[came, part], b_all.at[came, part], b_send.at[5 + n], b_recv.at[5 + n], goes
            )
        )
        b_far_sib.append(
            remote(
                b_all.at[y_far_row, part],
                b_all.at[y_far_row, part],
                b_send.at[9 + n],
                b_recv.at[9 + n],
                sibling,
            )
        )
    b_own_up.start()
    b_own_down.start()

    a_far = remote(a_ref, a_all.at[1], a_send.at[16], a_recv.at[1], x_far)
    a_up = remote(a_ref, a_all.at[2], a_send.at[14], a_recv.at[2], z_up)
    a_down = remote(a_ref, a_all.at[3], a_send.at[15], a_recv.at[3], z_down)
    a_far.start()
    a_up.start()
    a_down.start()
    b_own_sib.start()

    @pl.loop(1, N_ROW)
    def _(d):
        b_index_copy(d).start()

    @pl.loop(1, N_COL)
    def _(d):
        a_index_copy(d).start()

    def split_b(r, first=0, count=B_TILES):
        @pl.loop(first, first + count)
        def _(t):
            value = b_all[r, pl.ds(pl.multiple_of(t * TILE, TILE), TILE), :]
            hi = value.astype(jnp.bfloat16)
            b_hi[r * B_TILES + t] = hi
            b_lo[r * B_TILES + t] = (value - hi.astype(jnp.float32)).astype(jnp.bfloat16)

    def a_forward(k):
        ahead = (col + (1 - k % 2) * 2 + (k % 2) * (N_COL - 2)) % N_COL
        return remote(
            a_all.at[k], a_all.at[k + 4], a_send.at[k], a_recv.at[k + 4], at(row, ahead, layer)
        )

    def a_forward_half(k):
        ahead = (col + (1 - k % 2) * 2 + (k % 2) * (N_COL - 2)) % N_COL
        part = pl.ds(pl.multiple_of((k % 2) * HALF_A, HALF_A), HALF_A)
        return remote(
            a_all.at[k, part],
            a_all.at[14 + (k - 10) // 2, part],
            a_send.at[k],
            a_recv.at[k + 4],
            at(row, ahead, layer),
        )

    a_far_up = remote(a_all.at[1], a_all.at[4], a_send.at[0], a_recv.at[4], z_up)
    a_far_down = remote(a_all.at[1], a_all.at[5], a_send.at[1], a_recv.at[5], z_down)

    def a_arrival(k):
        return remote(a_all.at[k], a_all.at[k], a_send.at[k], a_recv.at[k], z_up)

    def a_arrival_half(k, n):
        part = pl.ds(n * HALF_A, HALF_A)
        return remote(
            a_all.at[k, part],
            a_all.at[k, part],
            a_send.at[k],
            a_recv.at[14 + 2 * (k - 14) + n],
            z_up,
        )

    b_local.wait()
    split_b(row)
    b_own_sib.wait_recv()
    split_b(sibling_row)
    for k in (2, 3):
        a_arrival(k).wait_recv()
        a_forward(k).start()
    @pl.loop(1, N_ROW)
    def _(d):
        b_index_copy(d).wait()

    @pl.loop(1, N_COL)
    def _(d):
        a_index_copy(d).wait()

    b_index = b_index_all[0]
    for r in range(1, N_ROW):
        b_index = jnp.maximum(b_index, b_index_all[r])
    panel = lane // SLOTS

    def one_row(i, found):
        a_index = a_index_all[i]
        for q in range(4):
            wanted = want[q, i]
            wanted_panel = wanted // 32 * 2 + wanted % 2
            match = (a_index == b_index) & (panel == wanted_panel)
            position = jnp.min(jnp.where(match, lane, B_ALL), axis=1, keepdims=True)
            found = jnp.where(lane == i * 4 + q, position, found)
        return found

    table_vmem[...] = lax.fori_loop(
        0, N_COL, one_row, jnp.full((8, TILE), B_ALL, jnp.int32), unroll=4
    )
    to_table = pltpu.make_async_copy(table_vmem, table, local_sem.at[2])
    to_table.start()
    to_table.wait()

    a_arrival(1).wait_recv()
    a_far_up.start()
    a_far_down.start()
    b_own_up.wait_recv()
    b_forward[0].start()
    b_forward[2].start()
    b_down_sib.start()
    b_own_down.wait_recv()
    b_forward[1].start()
    b_forward[3].start()
    b_up_sib.start()
    split_b(y_down_row)
    split_b(y_up_row)
    b_down_sib.wait_recv()
    split_b(sib_down)
    b_up_sib.wait_recv()
    split_b(sib_up)
    for k in (6, 7):
        a_arrival(k).wait_recv()
        a_forward(k).start()
    a_local.wait()
    for n in range(4):
        b_forward[n].wait_recv()
        b_far_sib[n].start()
    for tile, count in b_pieces:
        split_b(y_far_row, tile, count)
    for n, (tile, count) in enumerate(b_pieces):
        b_far_sib[n].wait_recv()
        split_b(sib_far, tile, count)

    def c_copy(k):
        return remote(
            to_send.at[k],
            arrived_ref.at[source_col(k, z, x_hi)],
            c_send.at[k],
            c_recv.at[k],
            partner,
        )

    def terms(i, half):
        for s in range(SLOTS):
            for n in range(2):
                t = table[s, i * 4 + half * 2 + n]
                rhs[0, s * TILE : (s + 1) * TILE, n * TILE : (n + 1) * TILE] = b_hi[t]
                rhs[1, s * TILE : (s + 1) * TILE, n * TILE : (n + 1) * TILE] = b_lo[t]
        both = jnp.dot(lhs[...], rhs[0], preferred_element_type=jnp.float32)
        low = jnp.dot(lhs[0:TILE, :], rhs[1], preferred_element_type=jnp.float32)
        return both[0:TILE] + (both[TILE : 2 * TILE] + low)

    @pl.loop(0, 16)
    def _(k):
        @pl.when(((k >= 4) & (k < 6)) | ((k >= 8) & (k < 14)))
        def _():
            a_arrival(k).wait_recv()

        @pl.when(((k >= 4) & (k < 6)) | ((k >= 8) & (k < 10)))
        def _():
            a_forward(k).start()

        @pl.when((k >= 10) & (k < 14))
        def _():
            a_forward_half(k).start()

        @pl.when(k >= 14)
        def _():
            a_arrival_half(k, 0).wait_recv()
            a_arrival_half(k, 1).wait_recv()

        i = source_col(k, z, x_hi)
        for s in range(SLOTS):
            value = a_all[k, s * TILE : (s + 1) * TILE, :]
            hi = value.astype(jnp.bfloat16)
            lhs[0:TILE, s * TILE : (s + 1) * TILE] = hi
            lhs[TILE : 2 * TILE, s * TILE : (s + 1) * TILE] = (
                value - hi.astype(jnp.float32)
            ).astype(jnp.bfloat16)
        theirs = terms(i, 1 - layer)
        to_send[k, 0] = theirs[:, 0:TILE]
        to_send[k, 1] = theirs[:, TILE : 2 * TILE]
        c_copy(k).start()
        ours = terms(i, layer)
        own_ref[i, 0] = ours[:, 0:TILE]
        own_ref[i, 1] = ours[:, TILE : 2 * TILE]

    for copy in (a_far, a_up, a_down, a_far_up, a_far_down):
        copy.wait_send()

    @pl.loop(2, 10)
    def _(k):
        a_forward(k).wait_send()

    @pl.loop(10, 14)
    def _(k):
        a_forward_half(k).wait_send()

    for copy in (b_own_up, b_own_down, b_own_sib, b_down_sib, b_up_sib, *b_forward, *b_far_sib):
        copy.wait_send()

    @pl.loop(0, 16)
    def _(k):
        c_copy(k).wait()


def on_device(a_tiles, a_cols, b_tiles, b_rows, c_cols):
    f32, i32, bf16 = jnp.float32, jnp.int32, jnp.bfloat16
    dma = pltpu.SemaphoreType.DMA
    in_hbm = pl.BlockSpec(memory_space=pltpu.HBM)
    in_vmem = pl.BlockSpec(memory_space=pltpu.VMEM)
    part = jax.ShapeDtypeStruct((16, 2, TILE, TILE), f32)
    own, arrived = pl.pallas_call(
        kernel,
        out_shape=(part, part),
        in_specs=[in_hbm] * 5,
        out_specs=(in_vmem, in_vmem),
        scratch_shapes=[
            pltpu.VMEM((16, A_ROWS, TILE), f32),
            pltpu.VMEM((N_ROW, B_ROWS, TILE), f32),
            pltpu.VMEM((B_ALL + 1, TILE, TILE), bf16),
            pltpu.VMEM((B_ALL + 1, TILE, TILE), bf16),
            pltpu.SMEM((4, N_COL), i32),
            pltpu.SMEM((1, 1, SLOTS), i32),
            pltpu.SMEM((2, 1, SLOTS), i32),
            pltpu.VMEM((N_COL, 8, TILE), i32),
            pltpu.VMEM((N_ROW, 8, TILE), i32),
            pltpu.VMEM((8, TILE), i32),
            pltpu.VMEM((8, TILE), i32),
            pltpu.VMEM((8, TILE), i32),
            pltpu.SMEM((8, TILE), i32),
            pltpu.VMEM((2 * TILE, A_ROWS), bf16),
            pltpu.VMEM((2, A_ROWS, 2 * TILE), bf16),
            pltpu.VMEM((16, 2, TILE, TILE), f32),
            dma((6,)),
            dma((N_COL,)),
            dma((N_COL,)),
            dma((N_ROW,)),
            dma((N_ROW,)),
            dma((17,)),
            dma((18,)),
            dma((13,)),
            dma((13,)),
            dma((16,)),
            dma((16,)),
        ],
        compiler_params=pltpu.CompilerParams(
            collective_id=0, has_side_effects=True, vmem_limit_bytes=48 * 2**20
        ),
        cost_estimate=pl.CostEstimate(
            flops=6 * 16 * 28 * TILE**3, bytes_accessed=4 * 2**20, transcendentals=0
        ),
        name="gather_multiply_sum",
    )(
        c_cols.reshape(16, 4).T,
        a_cols,
        b_rows,
        a_tiles.reshape(A_ROWS, TILE),
        b_tiles.reshape(B_ROWS, TILE),
    )
    return (own + arrived)[:, None]


def solution(mesh):
    return jax.shard_map(
        on_device,
        mesh=mesh,
        in_specs=(
            P(("row", "col"), "layer", None, None, None),
            P(("row", "col"), "layer", None),
            P(("row", "col"), "layer", None, None, None),
            P(("row", "col"), "layer", None),
            P("row", "col", None),
        ),
        out_specs=P("row", "col", "layer", None, None),
        check_vma=False,
    )
```

time: 103 us -> 104 us (level)
  local copies, waits for them, and re-layouts: 5.81 us -> 4.21 us
  Pallas kernels: 96 us -> 97.5 us
    broadcast_in_dim x0 -> x1, other arithmetic: none -> 1.57 us  [on_device(): return (own + arrived)[:, None]]
    pallas_call x1, Pallas kernels: 96 us -> 97.5 us  [on_device(): pl.pallas_call(kernel, out_shape=(part, part), in_specs=[in_hbm] * 5, out...]
    unnamed x1 -> x0, other arithmetic: 1.34 us -> none
    unnamed x6 -> x10, local copies, waits for them, and re-layouts: 4.03 us -> 4.21 us
where the time goes in v2:
time: 104 us; the launch traced here: 103 us
  Pallas kernels  97.5 us (94%)
  local copies, waits for them, and re-layouts  4.21 us (4%)
  other arithmetic  1.57 us (2%)
    pallas_call x1, Pallas kernels, on_device(): pl.pallas_call(kernel, out_shape=(part, part), in_specs=[in_hbm] * 5, out...  97.5 us
    unnamed x10, local copies, waits for them, and re-layouts  4.21 us

profile of v2, /device:TPU:1, one launch (start us, length us, event | category | flops | bytes accessed | tf_op | source)
XLA Modules:
  0.0 103.3 jit_solution(1808442302274965522)
XLA Ops:
  0.0 0.0 copy-start
  0.0 1.2 %copy-done = f32[2,1,7,128,128]{4,3,2,1,0:T(8,128)S(1)} copy-done((f32[2,1,7,128,128]{4,3,2,1,0:T(8,128)S(1)}, f32[2,1,7,128,128]{4,3,2,1,0:T(8,128)}, u32[]{:S(2)}) %copy-start) | copy-done | bytes 917528
  1.2 0.0 copy-start.1
  1.2 1.0 copy-done.1
  2.2 0.0 copy-start.2
  2.2 0.7 copy-done.2
  2.9 0.0 copy-start.3
  2.9 0.7 copy-done.3
  3.6 0.0 copy-start.4
  3.6 0.7 copy-done.4
  4.2 97.5 %gather_multiply_sum.1 = (f32[16,2,128,128]{3,2,1,0:T(8,128)S(1)}, f32[16,2,128,128]{3,2,1,0:T(8,128)S(1)}) custom-call(s32[4,16]{1,0:T(4,128)S(1)} %bitcast.11, s32[1,1,7]{2,1,0:T(1,128)S(1)} %copy-done.4, s32[2,1,7]{2,1,0:T(1,128)S(1)} %copy-done.3, f32[896,128]{1,0:T(8,128)S(1)} %bitcast.10, f32[1792,128]{1,0:T(8,128)S(1)} %bitcast.9), custom_call_target="tpu_custom_call" | custom-call | flops 5637144576 | bytes 4194304 | tf_op jit(solution)/shard_map/gather_multiply_sum/pallas_call | solution.py:389
  101.7 1.6 %add_bitcast_fusion = f32[16,1,2,128,128]{4,3,2,1,0:T(8,128)} fusion(f32[16,2,128,128]{3,2,1,0:T(8,128)S(1)} %get-tuple-element.7, f32[16,2,128,128]{3,2,1,0:T(8,128)S(1)} %get-tuple-element.8), kind=kLoop, calls=%fused_computation | loop fusion | flops 524288 | bytes 6291456 | tf_op jit(solution)/shard_map/broadcast_in_dim | solution.py:437
Async XLA Ops:
  0.0 1.2 %copy-start = (f32[2,1,7,128,128]{4,3,2,1,0:T(8,128)S(1)}, f32[2,1,7,128,128]{4,3,2,1,0:T(8,128)}, u32[]{:S(2)}) copy-start(f32[2,1,7,128,128]{4,3,2,1,0:T(8,128)} %param.7) | copy-start | bytes 2752516
  1.2 1.0 copy-start.1
  2.2 0.7 copy-start.2
  2.9 0.7 copy-start.3
  3.6 0.7 copy-start.4

commit v3 on v2

--- a/solution.py
+++ b/solution.py
@@ -118,6 +118,63 @@
         copy.start()
     b_local.start()
     a_local.start()
+    pl.semaphore_wait(barrier, N_COL + N_ROW - 1)
+
+    def a_index_copy(d):
+        return remote(
+            a_index_own,
+            a_index_all.at[col],
+            ai_send.at[d],
+            ai_recv.at[d],
+            at(row, (col + d) % N_COL, layer),
+        )
+
+    def b_index_copy(d):
+        return remote(
+            b_index_own,
+            b_index_all.at[row],
+            bi_send.at[d],
+            bi_recv.at[d],
+            at((row + d) % N_ROW, col, layer),
+        )
+
+    b_own_up = remote(b_ref, b_all.at[row], b_send.at[0], b_recv.at[0], y_up)
+    b_own_down = remote(b_ref, b_all.at[row], b_send.at[1], b_recv.at[1], y_down)
+    b_own_sib = remote(b_ref, b_all.at[row], b_send.at[2], b_recv.at[2], sibling)
+    b_down_sib = remote(
+        b_all.at[y_down_row], b_all.at[y_down_row], b_send.at[3], b_recv.at[3], sibling
+    )
+    b_up_sib = remote(b_all.at[y_up_row], b_all.at[y_up_row], b_send.at[4], b_recv.at[4], sibling)
+    b_pieces = ((0, 4), (7, 4), (4, 3), (11, 3))
+    b_forward, b_far_sib = [], []
+    for n, (tile, count) in enumerate(b_pieces):
+        part = pl.ds(tile * TILE, count * TILE)
+        came, goes = (y_down_row, y_up) if n % 2 == 0 else (y_up_row, y_down)
+        b_forward.append(
+            remote(
+                b_all.at[came, part], b_all.at[came, part], b_send.at[5 + n], b_recv.at[5 + n], goes
+            )
+        )
+        b_far_sib.append(
+            remote(
+                b_all.at[y_far_row, part],
+                b_all.at[y_far_row, part],
+                b_send.at[9 + n],
+                b_recv.at[9 + n],
+                sibling,
+            )
+        )
+    b_own_up.start()
+    b_own_down.start()
+
+    a_far = remote(a_ref, a_all.at[1], a_send.at[16], a_recv.at[1], x_far)
+    a_up = remote(a_ref, a_all.at[2], a_send.at[14], a_recv.at[2], z_up)
+    a_down = remote(a_ref, a_all.at[3], a_send.at[15], a_recv.at[3], z_down)
+    a_far.start()
+    a_up.start()
+    a_down.start()
+    b_own_sib.start()
+
     for copy in scalars:
         copy.wait()
     lane = lax.broadcasted_iota(jnp.int32, (8, TILE), 1)
@@ -134,62 +191,6 @@
     b_index_all[row] = b_index
     b_hi[B_ALL] = jnp.zeros((TILE, TILE), jnp.bfloat16)
     b_lo[B_ALL] = jnp.zeros((TILE, TILE), jnp.bfloat16)
-    pl.semaphore_wait(barrier, N_COL + N_ROW - 1)
-
-    def a_index_copy(d):
-        return remote(
-            a_index_own,
-            a_index_all.at[col],
-            ai_send.at[d],
-            ai_recv.at[d],
-            at(row, (col + d) % N_COL, layer),
-        )
-
-    def b_index_copy(d):
-        return remote(
-            b_index_own,
-            b_index_all.at[row],
-            bi_send.at[d],
-            bi_recv.at[d],
-            at((row + d) % N_ROW, col, layer),
-        )
-
-    b_own_up = remote(b_ref, b_all.at[row], b_send.at[0], b_recv.at[0], y_up)
-    b_own_down = remote(b_ref, b_all.at[row], b_send.at[1], b_recv.at[1], y_down)
-    b_own_sib = remote(b_ref, b_all.at[row], b_send.at[2], b_recv.at[2], sibling)
-    b_down_sib = remote(
-        b_all.at[y_down_row], b_all.at[y_down_row], b_send.at[3], b_recv.at[3], sibling
-    )
-    b_up_sib = remote(b_all.at[y_up_row], b_all.at[y_up_row], b_send.at[4], b_recv.at[4], sibling)
-    b_pieces = ((0, 4), (7, 4), (4, 3), (11, 3))
-    b_forward, b_far_sib = [], []
-    for n, (tile, count) in enumerate(b_pieces):
-        part = pl.ds(tile * TILE, count * TILE)
-        came, goes = (y_down_row, y_up) if n % 2 == 0 else (y_up_row, y_down)
-        b_forward.append(
-            remote(
-                b_all.at[came, part], b_all.at[came, part], b_send.at[5 + n], b_recv.at[5 + n], goes
-            )
-        )
-        b_far_sib.append(
-            remote(
-                b_all.at[y_far_row, part],
-                b_all.at[y_far_row, part],
-                b_send.at[9 + n],
-                b_recv.at[9 + n],
-                sibling,
-            )
-        )
-    b_own_up.start()
-    b_own_down.start()
-
-    a_far = remote(a_ref, a_all.at[1], a_send.at[16], a_recv.at[1], x_far)
-    a_up = remote(a_ref, a_all.at[2], a_send.at[14], a_recv.at[2], z_up)
-    a_down = remote(a_ref, a_all.at[3], a_send.at[15], a_recv.at[3], z_down)
-    a_far.start()
-    a_up.start()
-    a_down.start()
-    b_own_sib.start()
 
     @pl.loop(1, N_ROW)
     def _(d):
@@ -247,36 +248,6 @@
     for k in (2, 3):
         a_arrival(k).wait_recv()
         a_forward(k).start()
-    @pl.loop(1, N_ROW)
-    def _(d):
-        b_index_copy(d).wait()
-
-    @pl.loop(1, N_COL)
-    def _(d):
-        a_index_copy(d).wait()
-
-    b_index = b_index_all[0]
-    for r in range(1, N_ROW):
-        b_index = jnp.maximum(b_index, b_index_all[r])
-    panel = lane // SLOTS
-
-    def one_row(i, found):
-        a_index = a_index_all[i]
-        for q in range(4):
-            wanted = want[q, i]
-            wanted_panel = wanted // 32 * 2 + wanted % 2
-            match = (a_index == b_index) & (panel == wanted_panel)
-            position = jnp.min(jnp.where(match, lane, B_ALL), axis=1, keepdims=True)
-            found = jnp.where(lane == i * 4 + q, position, found)
-        return found
-
-    table_vmem[...] = lax.fori_loop(
-        0, N_COL, one_row, jnp.full((8, TILE), B_ALL, jnp.int32), unroll=4
-    )
-    to_table = pltpu.make_async_copy(table_vmem, table, local_sem.at[2])
-    to_table.start()
-    to_table.wait()
-
     a_arrival(1).wait_recv()
     a_far_up.start()
     a_far_down.start()
@@ -298,6 +269,36 @@
         a_arrival(k).wait_recv()
         a_forward(k).start()
     a_local.wait()
+    @pl.loop(1, N_ROW)
+    def _(d):
+        b_index_copy(d).wait()
+
+    @pl.loop(1, N_COL)
+    def _(d):
+        a_index_copy(d).wait()
+
+    b_index = b_index_all[0]
+    for r in range(1, N_ROW):
+        b_index = jnp.maximum(b_index, b_index_all[r])
+    panel = lane // SLOTS
+
+    def one_row(i, found):
+        a_index = a_index_all[i]
+        for q in range(4):
+            wanted = want[q, i]
+            wanted_panel = wanted // 32 * 2 + wanted % 2
+            match = (a_index == b_index) & (panel == wanted_panel)
+            position = jnp.min(jnp.where(match, lane, B_ALL), axis=1, keepdims=True)
+            found = jnp.where(lane == i * 4 + q, position, found)
+        return found
+
+    table_vmem[...] = lax.fori_loop(
+        0, N_COL, one_row, jnp.full((8, TILE), B_ALL, jnp.int32), unroll=4
+    )
+    to_table = pltpu.make_async_copy(table_vmem, table, local_sem.at[2])
+    to_table.start()
+    to_table.wait()
+
     for n in range(4):
         b_forward[n].wait_recv()
         b_far_sib[n].start()
@@ -378,6 +379,10 @@
     @pl.loop(0, 16)
     def _(k):
         c_copy(k).wait()
+
+
+def hbm(value):
+    return pltpu.with_memory_space_constraint(value, pltpu.HBM)
 
 
 def on_device(a_tiles, a_cols, b_tiles, b_rows, c_cols):
@@ -428,11 +433,11 @@
         ),
         name="gather_multiply_sum",
     )(
-        c_cols.reshape(16, 4).T,
-        a_cols,
-        b_rows,
-        a_tiles.reshape(A_ROWS, TILE),
-        b_tiles.reshape(B_ROWS, TILE),
+        hbm(c_cols.reshape(16, 4).T),
+        hbm(a_cols),
+        hbm(b_rows),
+        hbm(a_tiles.reshape(A_ROWS, TILE)),
+        hbm(b_tiles.reshape(B_ROWS, TILE)),
     )
     return (own + arrived)[:, None]
 

time: 104 us -> 95.3 us (0.916)
  local copies, waits for them, and re-layouts: 4.21 us -> 0 us
  Pallas kernels: 97.5 us -> 93.5 us
    unnamed x10 -> x0, local copies, waits for them, and re-layouts: 4.21 us -> none
    pallas_call x1, Pallas kernels: 97.5 us -> 93.5 us  [on_device(): pl.pallas_call(kernel, out_shape=(part, part), in_specs=[in_hbm] * 5, out...]
where the time goes in v3:
time: 95.3 us; the launch traced here: 95.2 us
  Pallas kernels  93.5 us (98%)
  other arithmetic  1.66 us (2%)
    pallas_call x1, Pallas kernels, on_device(): pl.pallas_call(kernel, out_shape=(part, part), in_specs=[in_hbm] * 5, out...  93.5 us

profile of v3, /device:TPU:1, one launch (start us, length us, event | category | flops | bytes accessed | tf_op | source)
XLA Modules:
  0.0 95.2 jit_solution(17713018024712292494)
XLA Ops:
  0.0 93.5 %gather_multiply_sum.1 = (f32[16,2,128,128]{3,2,1,0:T(8,128)S(1)}, f32[16,2,128,128]{3,2,1,0:T(8,128)S(1)}) custom-call(s32[4,16]{1,0:T(4,128)} %bitcast.11, s32[1,1,7]{2,1,0:T(1,128)} %a_cols_ref.1, s32[2,1,7]{2,1,0:T(1,128)} %b_rows_ref.1, f32[896,128]{1,0:T(8,128)} %bitcast.10, f32[1792,128]{1,0:T(8,128)} %bitcast.9), custom_call_target="tpu_custom_call" | custom-call | flops 5637144576 | bytes 4194304 | tf_op jit(solution)/shard_map/gather_multiply_sum/pallas_call | solution.py:394
  93.5 1.7 %add_bitcast_fusion = f32[16,1,2,128,128]{4,3,2,1,0:T(8,128)} fusion(f32[16,2,128,128]{3,2,1,0:T(8,128)S(1)} %get-tuple-element.7, f32[16,2,128,128]{3,2,1,0:T(8,128)S(1)} %get-tuple-element.8), kind=kLoop, calls=%fused_computation | loop fusion | flops 524288 | bytes 6291456 | tf_op jit(solution)/shard_map/broadcast_in_dim | solution.py:442

commit v4 on v3

--- a/solution.py
+++ b/solution.py
@@ -14,6 +14,7 @@
 N_ROW, N_COL = 8, 16
 B_ALL = N_ROW * B_TILES
 HALF_A = A_ROWS // 2
+HALF_B = B_ROWS // 2
 
 
 def source_col(k, z, x_hi):
@@ -40,7 +41,6 @@
     b_rows,
     a_index_all,
     b_index_all,
-    a_index_own,
     b_index_own,
     table_vmem,
     table,
@@ -48,6 +48,7 @@
     rhs,
     to_send,
     local_sem,
+    table_sem,
     ai_send,
     ai_recv,
     bi_send,
@@ -99,13 +100,8 @@
         )
     ]
 
+    before = 2 * (z % 2) + x_hi
     barrier = pltpu.get_barrier_semaphore()
-
-    @pl.loop(1, N_COL)
-    def _(d):
-        pl.semaphore_signal(
-            barrier, inc=1, device_id=at(row, (col + d) % N_COL, layer), device_id_type=MESH
-        )
 
     @pl.loop(1, N_ROW)
     def _(d):
@@ -118,16 +114,35 @@
         copy.start()
     b_local.start()
     a_local.start()
-    pl.semaphore_wait(barrier, N_COL + N_ROW - 1)
-
-    def a_index_copy(d):
-        return remote(
-            a_index_own,
-            a_index_all.at[col],
-            ai_send.at[d],
-            ai_recv.at[d],
-            at(row, (col + d) % N_COL, layer),
-        )
+    pl.semaphore_wait(barrier, N_ROW + before)
+
+    halves = (pl.ds(0, HALF_B), pl.ds(HALF_B, HALF_B))
+
+    def b_copy(r, part, n, device):
+        return remote(b_all.at[r, part], b_all.at[r, part], b_send.at[n], b_recv.at[n], device)
+
+    def b_own(half, n, device):
+        part = halves[half]
+        return remote(b_ref.at[part], b_all.at[row, part], b_send.at[n], b_recv.at[n], device)
+
+    b_own_up = [b_own(0, 0, y_up), b_own(1, 1, y_up)]
+    b_own_down = [b_own(1, 2, y_down), b_own(0, 3, y_down)]
+    b_own_sib = remote(b_ref, b_all.at[row], b_send.at[4], b_recv.at[4], sibling)
+    b_down_sib = [b_copy(y_down_row, halves[half], 5 + half, sibling) for half in (0, 1)]
+    b_up_sib = [b_copy(y_up_row, halves[half], 8 - half, sibling) for half in (1, 0)]
+    b_pieces = ((0, 4), (7, 4), (4, 3), (11, 3))
+    b_forward, b_far_sib = [], []
+    for n, (tile, count) in enumerate(b_pieces):
+        part = pl.ds(tile * TILE, count * TILE)
+        came, goes = (y_down_row, y_up) if n % 2 == 0 else (y_up_row, y_down)
+        b_forward.append(b_copy(came, part, 9 + n, goes))
+        b_far_sib.append(b_copy(y_far_row, part, 13 + n, sibling))
+    for n in range(2):
+        b_own_up[n].start()
+        b_own_down[n].start()
+    b_own_sib.start()
+    for device in (z_up, z_down, x_far):
+        pl.semaphore_signal(barrier, inc=1, device_id=device, device_id_type=MESH)
 
     def b_index_copy(d):
         return remote(
@@ -137,43 +152,6 @@
             bi_recv.at[d],
             at((row + d) % N_ROW, col, layer),
         )
-
-    b_own_up = remote(b_ref, b_all.at[row], b_send.at[0], b_recv.at[0], y_up)
-    b_own_down = remote(b_ref, b_all.at[row], b_send.at[1], b_recv.at[1], y_down)
-    b_own_sib = remote(b_ref, b_all.at[row], b_send.at[2], b_recv.at[2], sibling)
-    b_down_sib = remote(
-        b_all.at[y_down_row], b_all.at[y_down_row], b_send.at[3], b_recv.at[3], sibling
-    )
-    b_up_sib = remote(b_all.at[y_up_row], b_all.at[y_up_row], b_send.at[4], b_recv.at[4], sibling)
-    b_pieces = ((0, 4), (7, 4), (4, 3), (11, 3))
-    b_forward, b_far_sib = [], []
-    for n, (tile, count) in enumerate(b_pieces):
-        part = pl.ds(tile * TILE, count * TILE)
-        came, goes = (y_down_row, y_up) if n % 2 == 0 else (y_up_row, y_down)
-        b_forward.append(
-            remote(
-                b_all.at[came, part], b_all.at[came, part], b_send.at[5 + n], b_recv.at[5 + n], goes
-            )
-        )
-        b_far_sib.append(
-            remote(
-                b_all.at[y_far_row, part],
-                b_all.at[y_far_row, part],
-                b_send.at[9 + n],
-                b_recv.at[9 + n],
-                sibling,
-            )
-        )
-    b_own_up.start()
-    b_own_down.start()
-
-    a_far = remote(a_ref, a_all.at[1], a_send.at[16], a_recv.at[1], x_far)
-    a_up = remote(a_ref, a_all.at[2], a_send.at[14], a_recv.at[2], z_up)
-    a_down = remote(a_ref, a_all.at[3], a_send.at[15], a_recv.at[3], z_down)
-    a_far.start()
-    a_up.start()
-    a_down.start()
-    b_own_sib.start()
 
     for copy in scalars:
         copy.wait()
@@ -185,20 +163,53 @@
     b_index = jnp.full((8, TILE), -5, jnp.int32)
     for t in range(B_TILES):
         b_index = jnp.where(lane == row * B_TILES + t, b_rows[t // SLOTS, 0, t % SLOTS], b_index)
-    a_index_own[...] = a_index
     b_index_own[...] = b_index
-    a_index_all[col] = a_index
     b_index_all[row] = b_index
-    b_hi[B_ALL] = jnp.zeros((TILE, TILE), jnp.bfloat16)
-    b_lo[B_ALL] = jnp.zeros((TILE, TILE), jnp.bfloat16)
+    a_index_all[0] = a_index
 
     @pl.loop(1, N_ROW)
     def _(d):
         b_index_copy(d).start()
 
-    @pl.loop(1, N_COL)
-    def _(d):
-        a_index_copy(d).start()
+    class Both:
+        def __init__(self, *copies):
+            self.copies = copies
+
+        def start(self):
+            for copy in self.copies:
+                copy.start()
+
+        def wait_send(self):
+            for copy in self.copies:
+                copy.wait_send()
+
+    def a_index_copy(src, dst, n, device):
+        return remote(
+            a_index_all.at[src], a_index_all.at[dst], ai_send.at[n], ai_recv.at[dst], device
+        )
+
+    def a_copy(src, dst, n, device):
+        block = a_ref if src == 0 else a_all.at[src]
+        return Both(
+            a_index_copy(src, dst, n, device),
+            remote(block, a_all.at[dst], a_send.at[n], a_recv.at[dst], device),
+        )
+
+    a_first = [
+        a_copy(0, 2, 14, z_up),
+        a_copy(0, 3, 15, z_down),
+        a_copy(0, 1, 16, x_far),
+    ]
+    a_second = [a_copy(1, 4, 0, z_up), a_copy(1, 5, 1, z_down)]
+
+    @pl.when(before < 3)
+    def _():
+        pl.semaphore_wait(barrier, 3 - before)
+
+    for copy in a_first:
+        copy.start()
+    b_hi[B_ALL] = jnp.zeros((TILE, TILE), jnp.bfloat16)
+    b_lo[B_ALL] = jnp.zeros((TILE, TILE), jnp.bfloat16)
 
     def split_b(r, first=0, count=B_TILES):
         @pl.loop(first, first + count)
@@ -208,25 +219,30 @@
             b_hi[r * B_TILES + t] = hi
             b_lo[r * B_TILES + t] = (value - hi.astype(jnp.float32)).astype(jnp.bfloat16)
 
+    def ahead(k):
+        return at(row, (col + (1 - k % 2) * 2 + (k % 2) * (N_COL - 2)) % N_COL, layer)
+
+    def a_forward_index(k):
+        return a_index_copy(k, k + 4, k, ahead(k))
+
+    def a_forward_index_last(k):
+        return a_index_copy(k, 14 + (k - 10) // 2, k, ahead(k))
+
     def a_forward(k):
-        ahead = (col + (1 - k % 2) * 2 + (k % 2) * (N_COL - 2)) % N_COL
-        return remote(
-            a_all.at[k], a_all.at[k + 4], a_send.at[k], a_recv.at[k + 4], at(row, ahead, layer)
-        )
+        return remote(a_all.at[k], a_all.at[k + 4], a_send.at[k], a_recv.at[k + 4], ahead(k))
 
     def a_forward_half(k):
-        ahead = (col + (1 - k % 2) * 2 + (k % 2) * (N_COL - 2)) % N_COL
         part = pl.ds(pl.multiple_of((k % 2) * HALF_A, HALF_A), HALF_A)
         return remote(
             a_all.at[k, part],
             a_all.at[14 + (k - 10) // 2, part],
             a_send.at[k],
             a_recv.at[k + 4],
-            at(row, ahead, layer),
-        )
-
-    a_far_up = remote(a_all.at[1], a_all.at[4], a_send.at[0], a_recv.at[4], z_up)
-    a_far_down = remote(a_all.at[1], a_all.at[5], a_send.at[1], a_recv.at[5], z_down)
+            ahead(k),
+        )
+
+    def a_index_arrival(k):
+        return remote(a_index_all.at[k], a_index_all.at[k], ai_send.at[k], ai_recv.at[k], z_up)
 
     def a_arrival(k):
         return remote(a_all.at[k], a_all.at[k], a_send.at[k], a_recv.at[k], z_up)
@@ -241,67 +257,80 @@
             z_up,
         )
 
+    def table_copy(k):
+        return pltpu.make_async_copy(table_vmem.at[k], table.at[k], table_sem.at[k])
+
+    def make_table(k):
+        b_index = b_index_all[0]
+        for r in range(1, N_ROW):
+            b_index = jnp.maximum(b_index, b_index_all[r])
+        i = source_col(k, z, x_hi)
+        a_index = a_index_all[k]
+        found = jnp.full((8, TILE), B_ALL, jnp.int32)
+        for q in range(4):
+            wanted = want[q, i]
+            wanted_panel = wanted // 32 * 2 + wanted % 2
+            match = (a_index == b_index) & (lane // SLOTS == wanted_panel)
+            position = jnp.min(jnp.where(match, lane, B_ALL), axis=1, keepdims=True)
+            found = jnp.where(lane == q, position, found)
+        table_vmem[k] = found
+        table_copy(k).start()
+
     b_local.wait()
     split_b(row)
     b_own_sib.wait_recv()
     split_b(sibling_row)
     for k in (2, 3):
+        a_index_arrival(k).wait_recv()
+        a_forward_index(k).start()
         a_arrival(k).wait_recv()
         a_forward(k).start()
-    a_arrival(1).wait_recv()
-    a_far_up.start()
-    a_far_down.start()
-    b_own_up.wait_recv()
+    b_own_up[0].wait_recv()
     b_forward[0].start()
     b_forward[2].start()
-    b_down_sib.start()
-    b_own_down.wait_recv()
+    b_own_down[0].wait_recv()
     b_forward[1].start()
     b_forward[3].start()
-    b_up_sib.start()
+    b_down_sib[0].start()
+    b_up_sib[0].start()
+    b_own_up[1].wait_recv()
+    b_down_sib[1].start()
+    b_own_down[1].wait_recv()
+    b_up_sib[1].start()
+    a_index_arrival(1).wait_recv()
+    a_arrival(1).wait_recv()
+    for copy in a_second:
+        copy.start()
     split_b(y_down_row)
     split_b(y_up_row)
-    b_down_sib.wait_recv()
+    b_down_sib[0].wait_recv()
+    b_down_sib[1].wait_recv()
     split_b(sib_down)
-    b_up_sib.wait_recv()
+    b_up_sib[0].wait_recv()
+    b_up_sib[1].wait_recv()
     split_b(sib_up)
-    for k in (6, 7):
-        a_arrival(k).wait_recv()
-        a_forward(k).start()
-    a_local.wait()
+
     @pl.loop(1, N_ROW)
     def _(d):
         b_index_copy(d).wait()
 
-    @pl.loop(1, N_COL)
-    def _(d):
-        a_index_copy(d).wait()
-
-    b_index = b_index_all[0]
-    for r in range(1, N_ROW):
-        b_index = jnp.maximum(b_index, b_index_all[r])
-    panel = lane // SLOTS
-
-    def one_row(i, found):
-        a_index = a_index_all[i]
-        for q in range(4):
-            wanted = want[q, i]
-            wanted_panel = wanted // 32 * 2 + wanted % 2
-            match = (a_index == b_index) & (panel == wanted_panel)
-            position = jnp.min(jnp.where(match, lane, B_ALL), axis=1, keepdims=True)
-            found = jnp.where(lane == i * 4 + q, position, found)
-        return found
-
-    table_vmem[...] = lax.fori_loop(
-        0, N_COL, one_row, jnp.full((8, TILE), B_ALL, jnp.int32), unroll=4
-    )
-    to_table = pltpu.make_async_copy(table_vmem, table, local_sem.at[2])
-    to_table.start()
-    to_table.wait()
-
+    @pl.loop(0, 4)
+    def _(k):
+        make_table(k)
+
+    a_local.wait()
     for n in range(4):
         b_forward[n].wait_recv()
         b_far_sib[n].start()
+
+    @pl.loop(6, 8)
+    def _(k):
+        a_index_arrival(k).wait_recv()
+        a_forward_index(k).start()
+        a_arrival(k).wait_recv()
+        a_forward(k).start()
+        make_table(k)
+
     for tile, count in b_pieces:
         split_b(y_far_row, tile, count)
     for n, (tile, count) in enumerate(b_pieces):
@@ -317,10 +346,10 @@
             partner,
         )
 
-    def terms(i, half):
+    def terms(k, half):
         for s in range(SLOTS):
             for n in range(2):
-                t = table[s, i * 4 + half * 2 + n]
+                t = table[k, s, half * 2 + n]
                 rhs[0, s * TILE : (s + 1) * TILE, n * TILE : (n + 1) * TILE] = b_hi[t]
                 rhs[1, s * TILE : (s + 1) * TILE, n * TILE : (n + 1) * TILE] = b_lo[t]
         both = jnp.dot(lhs[...], rhs[0], preferred_element_type=jnp.float32)
@@ -329,15 +358,35 @@
 
     @pl.loop(0, 16)
     def _(k):
-        @pl.when(((k >= 4) & (k < 6)) | ((k >= 8) & (k < 14)))
+        full = ((k >= 4) & (k < 6)) | ((k >= 8) & (k < 10))
+        half = (k >= 10) & (k < 14)
+        late = ((k >= 4) & (k < 6)) | (k >= 8)
+
+        @pl.when(late)
+        def _():
+            a_index_arrival(k).wait_recv()
+
+        @pl.when(full)
+        def _():
+            a_forward_index(k).start()
+
+        @pl.when(half & (k % 2 == 0))
+        def _():
+            a_forward_index_last(k).start()
+
+        @pl.when(late)
+        def _():
+            make_table(k)
+
+        @pl.when(full | half)
         def _():
             a_arrival(k).wait_recv()
 
-        @pl.when(((k >= 4) & (k < 6)) | ((k >= 8) & (k < 10)))
+        @pl.when(full)
         def _():
             a_forward(k).start()
 
-        @pl.when((k >= 10) & (k < 14))
+        @pl.when(half)
         def _():
             a_forward_half(k).start()
 
@@ -354,26 +403,32 @@
             lhs[TILE : 2 * TILE, s * TILE : (s + 1) * TILE] = (
                 value - hi.astype(jnp.float32)
             ).astype(jnp.bfloat16)
-        theirs = terms(i, 1 - layer)
+        table_copy(k).wait()
+        theirs = terms(k, 1 - layer)
         to_send[k, 0] = theirs[:, 0:TILE]
         to_send[k, 1] = theirs[:, TILE : 2 * TILE]
         c_copy(k).start()
-        ours = terms(i, layer)
+        ours = terms(k, layer)
         own_ref[i, 0] = ours[:, 0:TILE]
         own_ref[i, 1] = ours[:, TILE : 2 * TILE]
 
-    for copy in (a_far, a_up, a_down, a_far_up, a_far_down):
+    for copy in (*a_first, *a_second):
         copy.wait_send()
 
     @pl.loop(2, 10)
     def _(k):
+        a_forward_index(k).wait_send()
         a_forward(k).wait_send()
 
     @pl.loop(10, 14)
     def _(k):
+        @pl.when(k % 2 == 0)
+        def _():
+            a_forward_index_last(k).wait_send()
+
         a_forward_half(k).wait_send()
 
-    for copy in (b_own_up, b_own_down, b_own_sib, b_down_sib, b_up_sib, *b_forward, *b_far_sib):
+    for copy in (*b_own_up, *b_own_down, b_own_sib, *b_down_sib, *b_up_sib, *b_forward, *b_far_sib):
         copy.wait_send()
 
     @pl.loop(0, 16)
@@ -404,24 +459,24 @@
             pltpu.SMEM((4, N_COL), i32),
             pltpu.SMEM((1, 1, SLOTS), i32),
             pltpu.SMEM((2, 1, SLOTS), i32),
-            pltpu.VMEM((N_COL, 8, TILE), i32),
+            pltpu.VMEM((16, 8, TILE), i32),
             pltpu.VMEM((N_ROW, 8, TILE), i32),
             pltpu.VMEM((8, TILE), i32),
-            pltpu.VMEM((8, TILE), i32),
-            pltpu.VMEM((8, TILE), i32),
-            pltpu.SMEM((8, TILE), i32),
+            pltpu.VMEM((16, 8, TILE), i32),
+            pltpu.SMEM((16, 8, TILE), i32),
             pltpu.VMEM((2 * TILE, A_ROWS), bf16),
             pltpu.VMEM((2, A_ROWS, 2 * TILE), bf16),
             pltpu.VMEM((16, 2, TILE, TILE), f32),
             dma((6,)),
-            dma((N_COL,)),
-            dma((N_COL,)),
+            dma((16,)),
+            dma((17,)),
+            dma((16,)),
             dma((N_ROW,)),
             dma((N_ROW,)),
             dma((17,)),
             dma((18,)),
-            dma((13,)),
-            dma((13,)),
+            dma((17,)),
+            dma((17,)),
             dma((16,)),
             dma((16,)),
         ],

time: 95.3 us -> 92.6 us (0.972)
  Pallas kernels: 93.5 us -> 90.1 us
    pallas_call x1, Pallas kernels: 93.5 us -> 90.1 us  [on_device(): pl.pallas_call(kernel, out_shape=(part, part), in_specs=[in_hbm] * 5, out...]
where the time goes in v4:
time: 92.6 us; the launch traced here: 91.7 us
  Pallas kernels  90.1 us (97%)
  other arithmetic  1.66 us (2%)
    pallas_call x1, Pallas kernels, on_device(): pl.pallas_call(kernel, out_shape=(part, part), in_specs=[in_hbm] * 5, out...  90.1 us

profile of v4, /device:TPU:1, one launch (start us, length us, event | category | flops | bytes accessed | tf_op | source)
XLA Modules:
  0.0 91.7 jit_solution(12403423458980484585)
XLA Ops:
  0.0 90.1 %gather_multiply_sum.1 = (f32[16,2,128,128]{3,2,1,0:T(8,128)S(1)}, f32[16,2,128,128]{3,2,1,0:T(8,128)S(1)}) custom-call(s32[4,16]{1,0:T(4,128)} %bitcast.11, s32[1,1,7]{2,1,0:T(1,128)} %a_cols_ref.1, s32[2,1,7]{2,1,0:T(1,128)} %b_rows_ref.1, f32[896,128]{1,0:T(8,128)} %bitcast.10, f32[1792,128]{1,0:T(8,128)} %bitcast.9), custom_call_target="tpu_custom_call" | custom-call | flops 5637144576 | bytes 4194304 | tf_op jit(solution)/shard_map/gather_multiply_sum/pallas_call | solution.py:449
  90.1 1.7 %add_bitcast_fusion = f32[16,1,2,128,128]{4,3,2,1,0:T(8,128)} fusion(f32[16,2,128,128]{3,2,1,0:T(8,128)S(1)} %get-tuple-element.7, f32[16,2,128,128]{3,2,1,0:T(8,128)S(1)} %get-tuple-element.8), kind=kLoop, calls=%fused_computation | loop fusion | flops 524288 | bytes 6291456 | tf_op jit(solution)/shard_map/broadcast_in_dim | solution.py:497

commit v5 on v4

--- a/solution.py
+++ b/solution.py
@@ -22,6 +22,12 @@
     other = (k // 2 + 1 + (15 - k) // 15 + k // 15) % 2
     sign = 2 * (k % 2) - 1
     return ((z + sign * distance + 8) % 8) * 2 + (x_hi + other) % 2
+
+
+def slot_of(n):
+    m = n % 4
+    third, fourth = (n // 8) * (1 - n // 12), n // 12
+    return n + third * (2 - 4 * (m // 2)) + fourth * (2 - 3 * ((m + 3) // 4) + m // 3)
 
 
 def kernel(
@@ -100,7 +106,7 @@
         )
     ]
 
-    before = 2 * (z % 2) + x_hi
+    before = (z + 7) // 8 + (z // 5) * (1 - z // 6) + x_hi
     barrier = pltpu.get_barrier_semaphore()
 
     @pl.loop(1, N_ROW)
@@ -130,13 +136,13 @@
     b_own_sib = remote(b_ref, b_all.at[row], b_send.at[4], b_recv.at[4], sibling)
     b_down_sib = [b_copy(y_down_row, halves[half], 5 + half, sibling) for half in (0, 1)]
     b_up_sib = [b_copy(y_up_row, halves[half], 8 - half, sibling) for half in (1, 0)]
-    b_pieces = ((0, 4), (7, 4), (4, 3), (11, 3))
+    b_pieces = ((0, 3), (7, 3), (3, 2), (10, 2), (5, 1), (12, 1), (6, 1), (13, 1))
     b_forward, b_far_sib = [], []
     for n, (tile, count) in enumerate(b_pieces):
         part = pl.ds(tile * TILE, count * TILE)
         came, goes = (y_down_row, y_up) if n % 2 == 0 else (y_up_row, y_down)
         b_forward.append(b_copy(came, part, 9 + n, goes))
-        b_far_sib.append(b_copy(y_far_row, part, 13 + n, sibling))
+        b_far_sib.append(b_copy(y_far_row, part, 17 + n, sibling))
     for n in range(2):
         b_own_up[n].start()
         b_own_down[n].start()
@@ -200,7 +206,7 @@
         a_copy(0, 3, 15, z_down),
         a_copy(0, 1, 16, x_far),
     ]
-    a_second = [a_copy(1, 4, 0, z_up), a_copy(1, 5, 1, z_down)]
+    a_second = [a_copy(1, 4, 0, z_up), a_copy(3, 5, 1, x_far)]
 
     @pl.when(before < 3)
     def _():
@@ -231,14 +237,13 @@
     def a_forward(k):
         return remote(a_all.at[k], a_all.at[k + 4], a_send.at[k], a_recv.at[k + 4], ahead(k))
 
+    def a_forward_last():
+        return remote(a_all.at[11], a_all.at[14], a_send.at[11], a_recv.at[14], ahead(11))
+
     def a_forward_half(k):
         part = pl.ds(pl.multiple_of((k % 2) * HALF_A, HALF_A), HALF_A)
         return remote(
-            a_all.at[k, part],
-            a_all.at[14 + (k - 10) // 2, part],
-            a_send.at[k],
-            a_recv.at[k + 4],
-            ahead(k),
+            a_all.at[k, part], a_all.at[15, part], a_send.at[k], a_recv.at[k + 3], ahead(k)
         )
 
     def a_index_arrival(k):
@@ -247,14 +252,10 @@
     def a_arrival(k):
         return remote(a_all.at[k], a_all.at[k], a_send.at[k], a_recv.at[k], z_up)
 
-    def a_arrival_half(k, n):
+    def a_arrival_half(n):
         part = pl.ds(n * HALF_A, HALF_A)
         return remote(
-            a_all.at[k, part],
-            a_all.at[k, part],
-            a_send.at[k],
-            a_recv.at[14 + 2 * (k - 14) + n],
-            z_up,
+            a_all.at[15, part], a_all.at[15, part], a_send.at[15], a_recv.at[15 + n], z_up
         )
 
     def table_copy(k):
@@ -285,24 +286,32 @@
         a_forward_index(k).start()
         a_arrival(k).wait_recv()
         a_forward(k).start()
+    a_second[1].start()
     b_own_up[0].wait_recv()
-    b_forward[0].start()
-    b_forward[2].start()
+    for copy in b_forward[0::2]:
+        copy.start()
     b_own_down[0].wait_recv()
-    b_forward[1].start()
-    b_forward[3].start()
+    for copy in b_forward[1::2]:
+        copy.start()
+    a_index_arrival(1).wait_recv()
+    a_arrival(1).wait_recv()
+    a_second[0].start()
     b_down_sib[0].start()
     b_up_sib[0].start()
     b_own_up[1].wait_recv()
     b_down_sib[1].start()
     b_own_down[1].wait_recv()
     b_up_sib[1].start()
-    a_index_arrival(1).wait_recv()
-    a_arrival(1).wait_recv()
-    for copy in a_second:
-        copy.start()
     split_b(y_down_row)
     split_b(y_up_row)
+
+    @pl.loop(6, 8)
+    def _(k):
+        a_index_arrival(k).wait_recv()
+        a_forward_index(k).start()
+        a_arrival(k).wait_recv()
+        a_forward(k).start()
+
     b_down_sib[0].wait_recv()
     b_down_sib[1].wait_recv()
     split_b(sib_down)
@@ -319,17 +328,9 @@
         make_table(k)
 
     a_local.wait()
-    for n in range(4):
+    for n in range(len(b_pieces)):
         b_forward[n].wait_recv()
         b_far_sib[n].start()
-
-    @pl.loop(6, 8)
-    def _(k):
-        a_index_arrival(k).wait_recv()
-        a_forward_index(k).start()
-        a_arrival(k).wait_recv()
-        a_forward(k).start()
-        make_table(k)
 
     for tile, count in b_pieces:
         split_b(y_far_row, tile, count)
@@ -357,43 +358,36 @@
         return both[0:TILE] + (both[TILE : 2 * TILE] + low)
 
     @pl.loop(0, 16)
-    def _(k):
-        full = ((k >= 4) & (k < 6)) | ((k >= 8) & (k < 10))
-        half = (k >= 10) & (k < 14)
-        late = ((k >= 4) & (k < 6)) | (k >= 8)
-
-        @pl.when(late)
-        def _():
-            a_index_arrival(k).wait_recv()
-
-        @pl.when(full)
-        def _():
-            a_forward_index(k).start()
-
-        @pl.when(half & (k % 2 == 0))
-        def _():
-            a_forward_index_last(k).start()
-
-        @pl.when(late)
-        def _():
-            make_table(k)
-
-        @pl.when(full | half)
-        def _():
-            a_arrival(k).wait_recv()
-
-        @pl.when(full)
-        def _():
-            a_forward(k).start()
-
-        @pl.when(half)
-        def _():
-            a_forward_half(k).start()
-
-        @pl.when(k >= 14)
-        def _():
-            a_arrival_half(k, 0).wait_recv()
-            a_arrival_half(k, 1).wait_recv()
+    def _(n):
+        k = slot_of(n)
+
+        @pl.when((n == 2) | (n == 10))
+        def _():
+            for j in (4, 5):
+                first = j + n // 10 * 4
+                a_arrival(first).wait_recv()
+                a_forward(first).start()
+
+        @pl.when(n == 6)
+        def _():
+            a_arrival(11).wait_recv()
+            a_forward_last().start()
+            a_arrival(10).wait_recv()
+
+        @pl.when(k == 14)
+        def _():
+            a_arrival(14).wait_recv()
+
+        @pl.when(k == 12)
+        def _():
+            for j in (12, 13):
+                a_arrival(j).wait_recv()
+                a_forward_half(j).start()
+
+        @pl.when(k == 15)
+        def _():
+            a_arrival_half(0).wait_recv()
+            a_arrival_half(1).wait_recv()
 
         i = source_col(k, z, x_hi)
         for s in range(SLOTS):
@@ -408,6 +402,25 @@
         to_send[k, 0] = theirs[:, 0:TILE]
         to_send[k, 1] = theirs[:, TILE : 2 * TILE]
         c_copy(k).start()
+
+        soon = slot_of(n + 1)
+
+        @pl.when((soon < 16) & ((soon >= 8) | ((soon >= 4) & (soon < 6))))
+        def _():
+            a_index_arrival(soon).wait_recv()
+
+        @pl.when(((soon >= 4) & (soon < 6)) | ((soon >= 8) & (soon < 10)))
+        def _():
+            a_forward_index(soon).start()
+
+        @pl.when((soon == 11) | (soon == 12))
+        def _():
+            a_forward_index_last(soon).start()
+
+        @pl.when((soon >= 4) & (soon < 16))
+        def _():
+            make_table(soon)
+
         ours = terms(k, layer)
         own_ref[i, 0] = ours[:, 0:TILE]
         own_ref[i, 1] = ours[:, TILE : 2 * TILE]
@@ -420,14 +433,11 @@
         a_forward_index(k).wait_send()
         a_forward(k).wait_send()
 
-    @pl.loop(10, 14)
-    def _(k):
-        @pl.when(k % 2 == 0)
-        def _():
-            a_forward_index_last(k).wait_send()
-
-        a_forward_half(k).wait_send()
-
+    a_forward_index_last(11).wait_send()
+    a_forward_index_last(12).wait_send()
+    a_forward_last().wait_send()
+    a_forward_half(12).wait_send()
+    a_forward_half(13).wait_send()
     for copy in (*b_own_up, *b_own_down, b_own_sib, *b_down_sib, *b_up_sib, *b_forward, *b_far_sib):
         copy.wait_send()
 
@@ -475,8 +485,8 @@
             dma((N_ROW,)),
             dma((17,)),
             dma((18,)),
-            dma((17,)),
-            dma((17,)),
+            dma((25,)),
+            dma((25,)),
             dma((16,)),
             dma((16,)),
         ],

time: 92.6 us -> 90.4 us (0.976)
  Pallas kernels: 90.1 us -> 87.1 us
    pallas_call x1, Pallas kernels: 90.1 us -> 87.1 us  [on_device(): pl.pallas_call(kernel, out_shape=(part, part), in_specs=[in_hbm] * 5, out...]
where the time goes in v5:
time: 90.4 us; the launch traced here: 88.7 us
  Pallas kernels  87.1 us (96%)
  other arithmetic  1.66 us (2%)
    pallas_call x1, Pallas kernels, on_device(): pl.pallas_call(kernel, out_shape=(part, part), in_specs=[in_hbm] * 5, out...  87.1 us

profile of v5, /device:TPU:1, one launch (start us, length us, event | category | flops | bytes accessed | tf_op | source)
XLA Modules:
  0.0 88.7 jit_solution(6655326306238145021)
XLA Ops:
  0.0 87.1 %gather_multiply_sum.1 = (f32[16,2,128,128]{3,2,1,0:T(8,128)S(1)}, f32[16,2,128,128]{3,2,1,0:T(8,128)S(1)}) custom-call(s32[4,16]{1,0:T(4,128)} %bitcast.11, s32[1,1,7]{2,1,0:T(1,128)} %a_cols_ref.1, s32[2,1,7]{2,1,0:T(1,128)} %b_rows_ref.1, f32[896,128]{1,0:T(8,128)} %bitcast.10, f32[1792,128]{1,0:T(8,128)} %bitcast.9), custom_call_target="tpu_custom_call" | custom-call | flops 5637144576 | bytes 4194304 | tf_op jit(solution)/shard_map/gather_multiply_sum/pallas_call | solution.py:459
  87.1 1.7 %add_bitcast_fusion = f32[16,1,2,128,128]{4,3,2,1,0:T(8,128)} fusion(f32[16,2,128,128]{3,2,1,0:T(8,128)S(1)} %get-tuple-element.7, f32[16,2,128,128]{3,2,1,0:T(8,128)S(1)} %get-tuple-element.8), kind=kLoop, calls=%fused_computation | loop fusion | flops 524288 | bytes 6291456 | tf_op jit(solution)/shard_map/broadcast_in_dim | solution.py:507

commit v6 on v5

--- a/solution.py
+++ b/solution.py
@@ -106,7 +106,8 @@
         )
     ]
 
-    before = (z + 7) // 8 + (z // 5) * (1 - z // 6) + x_hi
+    is_4, is_5, is_6 = ((z // v) * (1 - z // (v + 1)) for v in (4, 5, 6))
+    before = (z + 7) // 8 + is_4 - is_5 + is_6 + x_hi
     barrier = pltpu.get_barrier_semaphore()
 
     @pl.loop(1, N_ROW)
@@ -257,6 +258,49 @@
         return remote(
             a_all.at[15, part], a_all.at[15, part], a_send.at[15], a_recv.at[15 + n], z_up
         )
+
+    def load_block(n):
+        k = slot_of(n)
+
+        @pl.when(n == 2)
+        def _():
+            a_arrival(4).wait_recv()
+            a_forward(4).start()
+
+        @pl.when(n == 10)
+        def _():
+            for j in (8, 9):
+                a_arrival(j).wait_recv()
+                a_forward(j).start()
+
+        @pl.when(n == 6)
+        def _():
+            a_arrival(11).wait_recv()
+            a_forward_last().start()
+            a_arrival(10).wait_recv()
+
+        @pl.when(k == 14)
+        def _():
+            a_arrival(14).wait_recv()
+
+        @pl.when(k == 12)
+        def _():
+            for j in (12, 13):
+                a_arrival(j).wait_recv()
+                a_forward_half(j).start()
+
+        @pl.when(k == 15)
+        def _():
+            a_arrival_half(0).wait_recv()
+            a_arrival_half(1).wait_recv()
+
+        for s in range(SLOTS):
+            value = a_all[k, s * TILE : (s + 1) * TILE, :]
+            hi = value.astype(jnp.bfloat16)
+            lhs[0:TILE, s * TILE : (s + 1) * TILE] = hi
+            lhs[TILE : 2 * TILE, s * TILE : (s + 1) * TILE] = (
+                value - hi.astype(jnp.float32)
+            ).astype(jnp.bfloat16)
 
     def table_copy(k):
         return pltpu.make_async_copy(table_vmem.at[k], table.at[k], table_sem.at[k])
@@ -327,7 +371,12 @@
     def _(k):
         make_table(k)
 
+    a_index_arrival(5).wait_recv()
+    a_forward_index(5).start()
+    a_arrival(5).wait_recv()
+    a_forward(5).start()
     a_local.wait()
+    load_block(0)
     for n in range(len(b_pieces)):
         b_forward[n].wait_recv()
         b_far_sib[n].start()
@@ -360,43 +409,7 @@
     @pl.loop(0, 16)
     def _(n):
         k = slot_of(n)
-
-        @pl.when((n == 2) | (n == 10))
-        def _():
-            for j in (4, 5):
-                first = j + n // 10 * 4
-                a_arrival(first).wait_recv()
-                a_forward(first).start()
-
-        @pl.when(n == 6)
-        def _():
-            a_arrival(11).wait_recv()
-            a_forward_last().start()
-            a_arrival(10).wait_recv()
-
-        @pl.when(k == 14)
-        def _():
-            a_arrival(14).wait_recv()
-
-        @pl.when(k == 12)
-        def _():
-            for j in (12, 13):
-                a_arrival(j).wait_recv()
-                a_forward_half(j).start()
-
-        @pl.when(k == 15)
-        def _():
-            a_arrival_half(0).wait_recv()
-            a_arrival_half(1).wait_recv()
-
         i = source_col(k, z, x_hi)
-        for s in range(SLOTS):
-            value = a_all[k, s * TILE : (s + 1) * TILE, :]
-            hi = value.astype(jnp.bfloat16)
-            lhs[0:TILE, s * TILE : (s + 1) * TILE] = hi
-            lhs[TILE : 2 * TILE, s * TILE : (s + 1) * TILE] = (
-                value - hi.astype(jnp.float32)
-            ).astype(jnp.bfloat16)
         table_copy(k).wait()
         theirs = terms(k, 1 - layer)
         to_send[k, 0] = theirs[:, 0:TILE]
@@ -405,11 +418,11 @@
 
         soon = slot_of(n + 1)
 
-        @pl.when((soon < 16) & ((soon >= 8) | ((soon >= 4) & (soon < 6))))
+        @pl.when((soon == 4) | ((soon >= 8) & (soon < 16)))
         def _():
             a_index_arrival(soon).wait_recv()
 
-        @pl.when(((soon >= 4) & (soon < 6)) | ((soon >= 8) & (soon < 10)))
+        @pl.when((soon == 4) | (soon == 8) | (soon == 9))
         def _():
             a_forward_index(soon).start()
 
@@ -424,6 +437,10 @@
         ours = terms(k, layer)
         own_ref[i, 0] = ours[:, 0:TILE]
         own_ref[i, 1] = ours[:, TILE : 2 * TILE]
+
+        @pl.when(n < 15)
+        def _():
+            load_block(n + 1)
 
     for copy in (*a_first, *a_second):
         copy.wait_send()
@@ -444,6 +461,17 @@
     @pl.loop(0, 16)
     def _(k):
         c_copy(k).wait()
+
+
+def add_kernel(own_ref, arrived_ref, out_ref, total, sem):
+    copies = []
+    for n in range(4):
+        part = pl.ds(4 * n, 4)
+        total[part] = own_ref[part] + arrived_ref[part]
+        copies.append(pltpu.make_async_copy(total.at[part], out_ref.at[part], sem.at[n]))
+        copies[-1].start()
+    for copy in copies:
+        copy.wait()
 
 
 def hbm(value):
@@ -504,7 +532,16 @@
         hbm(a_tiles.reshape(A_ROWS, TILE)),
         hbm(b_tiles.reshape(B_ROWS, TILE)),
     )
-    return (own + arrived)[:, None]
+    out = pl.pallas_call(
+        add_kernel,
+        out_shape=part,
+        in_specs=[in_vmem, in_vmem],
+        out_specs=in_hbm,
+        scratch_shapes=[pltpu.VMEM((16, 2, TILE, TILE), f32), dma((4,))],
+        compiler_params=pltpu.CompilerParams(vmem_limit_bytes=8 * 2**20),
+        name="add_halves",
+    )(own, arrived)
+    return out[:, None]
 
 
 def solution(mesh):

time: 90.4 us -> 89 us (0.985); the launches traced: 88.7 us -> 88.4 us
  other arithmetic: 1.66 us -> 0 us
  Pallas kernels: 87.1 us -> 88.3 us
    broadcast_in_dim x1 -> x0, other arithmetic: 1.66 us -> none  [on_device(): return (own + arrived)[:, None]]
    pallas_call x0 -> x1, Pallas kernels: none -> 1.4 us  [on_device(): pl.pallas_call(add_kernel, out_shape=part, in_specs=[in_vmem, in_vmem], o...]
where the time goes in v6:
time: 89 us; the launch traced here: 88.4 us
  Pallas kernels  88.3 us (99%)
    pallas_call x1, Pallas kernels, on_device(): pl.pallas_call(kernel, out_shape=(part, part), in_specs=[in_hbm] * 5, out...  86.9 us

profile of v6, /device:TPU:1, one launch (start us, length us, event | category | flops | bytes accessed | tf_op | source)
XLA Modules:
  0.0 88.4 jit_solution(16500717166479282327)
XLA Ops:
  0.0 86.9 %gather_multiply_sum.1 = (f32[16,2,128,128]{3,2,1,0:T(8,128)S(1)}, f32[16,2,128,128]{3,2,1,0:T(8,128)S(1)}) custom-call(s32[4,16]{1,0:T(4,128)} %bitcast.10, s32[1,1,7]{2,1,0:T(1,128)} %a_cols_ref.1, s32[2,1,7]{2,1,0:T(1,128)} %b_rows_ref.1, f32[896,128]{1,0:T(8,128)} %bitcast.9, f32[1792,128]{1,0:T(8,128)} %bitcast.8), custom_call_target="tpu_custom_call" | custom-call | flops 5637144576 | bytes 4194304 | tf_op jit(solution)/shard_map/gather_multiply_sum/pallas_call | solution.py:487
  87.0 1.4 %add_halves.1 = f32[16,2,128,128]{3,2,1,0:T(8,128)} custom-call(f32[16,2,128,128]{3,2,1,0:T(8,128)S(1)} %get-tuple-element.7.own_ref, f32[16,2,128,128]{3,2,1,0:T(8,128)S(1)} %get-tuple-element.8.arrived_ref), custom_call_target="tpu_custom_call" | custom-call | tf_op jit(solution)/shard_map/add_halves/pallas_call | solution.py:535

commit v7 on v6

--- a/solution.py
+++ b/solution.py
@@ -65,6 +65,7 @@
     b_recv,
     c_send,
     c_recv,
+    answers,
 ):
     row, col, layer = lax.axis_index("row"), lax.axis_index("col"), lax.axis_index("layer")
     z, x_hi = col // 2, col % 2
@@ -106,22 +107,36 @@
         )
     ]
 
-    is_4, is_5, is_6 = ((z // v) * (1 - z // (v + 1)) for v in (4, 5, 6))
-    before = (z + 7) // 8 + is_4 - is_5 + is_6 + x_hi
+    other = (core + 1) % 2
+    pairs = (
+        (z_up, (z < 4) | (z == 5)),
+        (z_down, (z == 0) | (z == 5) | (z == 7)),
+        (x_far, x_hi == 0),
+        (partner, layer == 0),
+        (at(y_far_row, col, layer), y < 2),
+        (at((y + 2) % 4 * 2 + other, col, layer), y < 2),
+        (at((y + 1) % 4 * 2 + other, col, layer), y < 3),
+        (at((y + 3) % 4 * 2 + other, col, layer), y == 0),
+    )
+    is_0, is_4, is_5, is_6 = (
+        (z + 8 - v) // 8 * (1 - (z + 7 - v) // 8) for v in (0, 4, 5, 6)
+    )
+    before = 1 - is_0 + is_4 - is_5 + is_6 + x_hi + layer + 2 * (y // 2) + (y + 1) // 2
+    after = len(pairs) - before
     barrier = pltpu.get_barrier_semaphore()
-
-    @pl.loop(1, N_ROW)
-    def _(d):
-        pl.semaphore_signal(
-            barrier, inc=1, device_id=at((row + d) % N_ROW, col, layer), device_id_type=MESH
-        )
-
-    pl.semaphore_signal(barrier, inc=1, device_id=partner, device_id_type=MESH)
+    for device in (y_up, y_down, sibling):
+        pl.semaphore_signal(barrier, inc=1, device_id=device, device_id_type=MESH)
+    for device, first in pairs:
+
+        @pl.when(first)
+        def _():
+            pl.semaphore_signal(barrier, inc=1, device_id=device, device_id_type=MESH)
+
     for copy in scalars:
         copy.start()
     b_local.start()
     a_local.start()
-    pl.semaphore_wait(barrier, N_ROW + before)
+    pl.semaphore_wait(barrier, 3 + before)
 
     halves = (pl.ds(0, HALF_B), pl.ds(HALF_B, HALF_B))
 
@@ -148,8 +163,12 @@
         b_own_up[n].start()
         b_own_down[n].start()
     b_own_sib.start()
-    for device in (z_up, z_down, x_far):
-        pl.semaphore_signal(barrier, inc=1, device_id=device, device_id_type=MESH)
+    for device, first in pairs:
+
+        @pl.when(jnp.logical_not(first))
+        def _():
+            pl.semaphore_signal(answers, inc=1, device_id=device, device_id_type=MESH)
+
 
     def b_index_copy(d):
         return remote(
@@ -174,10 +193,6 @@
     b_index_all[row] = b_index
     a_index_all[0] = a_index
 
-    @pl.loop(1, N_ROW)
-    def _(d):
-        b_index_copy(d).start()
-
     class Both:
         def __init__(self, *copies):
             self.copies = copies
@@ -209,12 +224,17 @@
     ]
     a_second = [a_copy(1, 4, 0, z_up), a_copy(3, 5, 1, x_far)]
 
-    @pl.when(before < 3)
+    @pl.when(after > 0)
     def _():
-        pl.semaphore_wait(barrier, 3 - before)
+        pl.semaphore_wait(answers, after)
 
     for copy in a_first:
         copy.start()
+
+    @pl.loop(1, N_ROW)
+    def _(d):
+        b_index_copy(d).start()
+
     b_hi[B_ALL] = jnp.zeros((TILE, TILE), jnp.bfloat16)
     b_lo[B_ALL] = jnp.zeros((TILE, TILE), jnp.bfloat16)
 
@@ -325,12 +345,13 @@
     split_b(row)
     b_own_sib.wait_recv()
     split_b(sibling_row)
-    for k in (2, 3):
+    for k in (3, 2):
         a_index_arrival(k).wait_recv()
         a_forward_index(k).start()
         a_arrival(k).wait_recv()
         a_forward(k).start()
-    a_second[1].start()
+        if k == 3:
+            a_second[1].start()
     b_own_up[0].wait_recv()
     for copy in b_forward[0::2]:
         copy.start()
@@ -517,6 +538,7 @@
             dma((25,)),
             dma((16,)),
             dma((16,)),
+            pltpu.SemaphoreType.REGULAR,
         ],
         compiler_params=pltpu.CompilerParams(
             collective_id=0, has_side_effects=True, vmem_limit_bytes=48 * 2**20

time: 89 us -> 88.5 us (level)
  Pallas kernels: 88.3 us -> 87.3 us
    pallas_call x1, Pallas kernels: 86.9 us -> 85.9 us  [on_device(): pl.pallas_call(kernel, out_shape=(part, part), in_specs=[in_hbm] * 5, out...]
where the time goes in v7:
time: 88.5 us; the launch traced here: 87.3 us
  Pallas kernels  87.3 us (99%)
    pallas_call x1, Pallas kernels, on_device(): pl.pallas_call(kernel, out_shape=(part, part), in_specs=[in_hbm] * 5, out...  85.9 us

profile of v7, /device:TPU:1, one launch (start us, length us, event | category | flops | bytes accessed | tf_op | source)
XLA Modules:
  0.0 87.3 jit_solution(2052863244807871656)
XLA Ops:
  0.0 85.9 %gather_multiply_sum.1 = (f32[16,2,128,128]{3,2,1,0:T(8,128)S(1)}, f32[16,2,128,128]{3,2,1,0:T(8,128)S(1)}) custom-call(s32[4,16]{1,0:T(4,128)} %bitcast.10, s32[1,1,7]{2,1,0:T(1,128)} %a_cols_ref.1, s32[2,1,7]{2,1,0:T(1,128)} %b_rows_ref.1, f32[896,128]{1,0:T(8,128)} %bitcast.9, f32[1792,128]{1,0:T(8,128)} %bitcast.8), custom_call_target="tpu_custom_call" | custom-call | flops 5637144576 | bytes 4194304 | tf_op jit(solution)/shard_map/gather_multiply_sum/pallas_call | solution.py:508
  85.9 1.4 %add_halves.1 = f32[16,2,128,128]{3,2,1,0:T(8,128)} custom-call(f32[16,2,128,128]{3,2,1,0:T(8,128)S(1)} %get-tuple-element.7.own_ref, f32[16,2,128,128]{3,2,1,0:T(8,128)S(1)} %get-tuple-element.8.arrived_ref), custom_call_target="tpu_custom_call" | custom-call | tf_op jit(solution)/shard_map/add_halves/pallas_call | solution.py:557

commit v8 on v7

--- a/solution.py
+++ b/solution.py
@@ -289,7 +289,7 @@
 
         @pl.when(n == 10)
         def _():
-            for j in (8, 9):
+            for j in (9, 8):
                 a_arrival(j).wait_recv()
                 a_forward(j).start()
 
@@ -297,6 +297,9 @@
         def _():
             a_arrival(11).wait_recv()
             a_forward_last().start()
+
+        @pl.when(n == 8)
+        def _():
             a_arrival(10).wait_recv()
 
         @pl.when(k == 14)
@@ -305,7 +308,7 @@
 
         @pl.when(k == 12)
         def _():
-            for j in (12, 13):
+            for j in (13, 12):
                 a_arrival(j).wait_recv()
                 a_forward_half(j).start()
 

time: 88.5 us -> 88.5 us (level)
  no operation moved by 1% of the time
where the time goes in v8:
time: 88.5 us; the launch traced here: 87.3 us
  Pallas kernels  87.3 us (99%)
    pallas_call x1, Pallas kernels, on_device(): pl.pallas_call(kernel, out_shape=(part, part), in_specs=[in_hbm] * 5, out...  85.9 us

profile of v8, /device:TPU:1, one launch (start us, length us, event | category | flops | bytes accessed | tf_op | source)
XLA Modules:
  0.0 87.3 jit_solution(7507913905357108316)
XLA Ops:
  0.0 85.9 %gather_multiply_sum.1 = (f32[16,2,128,128]{3,2,1,0:T(8,128)S(1)}, f32[16,2,128,128]{3,2,1,0:T(8,128)S(1)}) custom-call(s32[4,16]{1,0:T(4,128)} %bitcast.10, s32[1,1,7]{2,1,0:T(1,128)} %a_cols_ref.1, s32[2,1,7]{2,1,0:T(1,128)} %b_rows_ref.1, f32[896,128]{1,0:T(8,128)} %bitcast.9, f32[1792,128]{1,0:T(8,128)} %bitcast.8), custom_call_target="tpu_custom_call" | custom-call | flops 5637144576 | bytes 4194304 | tf_op jit(solution)/shard_map/gather_multiply_sum/pallas_call | solution.py:511
  85.9 1.4 %add_halves.1 = f32[16,2,128,128]{3,2,1,0:T(8,128)} custom-call(f32[16,2,128,128]{3,2,1,0:T(8,128)S(1)} %get-tuple-element.7.own_ref, f32[16,2,128,128]{3,2,1,0:T(8,128)S(1)} %get-tuple-element.8.arrived_ref), custom_call_target="tpu_custom_call" | custom-call | tf_op jit(solution)/shard_map/add_halves/pallas_call | solution.py:560

commit v9 on v8

--- a/solution.py
+++ b/solution.py
@@ -411,23 +411,24 @@
         b_far_sib[n].wait_recv()
         split_b(sib_far, tile, count)
 
-    def c_copy(k):
+    def c_copy(k, n):
         return remote(
-            to_send.at[k],
-            arrived_ref.at[source_col(k, z, x_hi)],
-            c_send.at[k],
-            c_recv.at[k],
+            to_send.at[k, n],
+            arrived_ref.at[source_col(k, z, x_hi), n],
+            c_send.at[k, n],
+            c_recv.at[k, n],
             partner,
         )
 
-    def terms(k, half):
+    def gather(k, half, n):
         for s in range(SLOTS):
-            for n in range(2):
-                t = table[k, s, half * 2 + n]
-                rhs[0, s * TILE : (s + 1) * TILE, n * TILE : (n + 1) * TILE] = b_hi[t]
-                rhs[1, s * TILE : (s + 1) * TILE, n * TILE : (n + 1) * TILE] = b_lo[t]
-        both = jnp.dot(lhs[...], rhs[0], preferred_element_type=jnp.float32)
-        low = jnp.dot(lhs[0:TILE, :], rhs[1], preferred_element_type=jnp.float32)
+            t = table[k, s, half * 2 + n]
+            rhs[0, s * TILE : (s + 1) * TILE, n * TILE : (n + 1) * TILE] = b_hi[t]
+            rhs[1, s * TILE : (s + 1) * TILE, n * TILE : (n + 1) * TILE] = b_lo[t]
+
+    def product(columns):
+        both = jnp.dot(lhs[...], rhs[0, :, columns], preferred_element_type=jnp.float32)
+        low = jnp.dot(lhs[0:TILE, :], rhs[1, :, columns], preferred_element_type=jnp.float32)
         return both[0:TILE] + (both[TILE : 2 * TILE] + low)
 
     @pl.loop(0, 16)
@@ -435,10 +436,10 @@
         k = slot_of(n)
         i = source_col(k, z, x_hi)
         table_copy(k).wait()
-        theirs = terms(k, 1 - layer)
-        to_send[k, 0] = theirs[:, 0:TILE]
-        to_send[k, 1] = theirs[:, TILE : 2 * TILE]
-        c_copy(k).start()
+        for m in range(2):
+            gather(k, 1 - layer, m)
+            to_send[k, m] = product(slice(m * TILE, (m + 1) * TILE))
+            c_copy(k, m).start()
 
         soon = slot_of(n + 1)
 
@@ -458,7 +459,9 @@
         def _():
             make_table(soon)
 
-        ours = terms(k, layer)
+        gather(k, layer, 0)
+        gather(k, layer, 1)
+        ours = product(slice(0, 2 * TILE))
         own_ref[i, 0] = ours[:, 0:TILE]
         own_ref[i, 1] = ours[:, TILE : 2 * TILE]
 
@@ -484,7 +487,8 @@
 
     @pl.loop(0, 16)
     def _(k):
-        c_copy(k).wait()
+        c_copy(k, 0).wait()
+        c_copy(k, 1).wait()
 
 
 def add_kernel(own_ref, arrived_ref, out_ref, total, sem):
@@ -539,8 +543,8 @@
             dma((18,)),
             dma((25,)),
             dma((25,)),
-            dma((16,)),
-            dma((16,)),
+            dma((16, 2)),
+            dma((16, 2)),
             pltpu.SemaphoreType.REGULAR,
         ],
         compiler_params=pltpu.CompilerParams(

time: 88.5 us -> 88.7 us (level)
  no operation moved by 1% of the time
where the time goes in v9:
time: 88.7 us; the launch traced here: 87.5 us
  Pallas kernels  87.5 us (99%)
    pallas_call x1, Pallas kernels, on_device(): pl.pallas_call(kernel, out_shape=(part, part), in_specs=[in_hbm] * 5, out...  86.1 us

profile of v9, /device:TPU:1, one launch (start us, length us, event | category | flops | bytes accessed | tf_op | source)
XLA Modules:
  0.0 87.5 jit_solution(16145772502434035098)
XLA Ops:
  0.0 86.1 %gather_multiply_sum.1 = (f32[16,2,128,128]{3,2,1,0:T(8,128)S(1)}, f32[16,2,128,128]{3,2,1,0:T(8,128)S(1)}) custom-call(s32[4,16]{1,0:T(4,128)} %bitcast.10, s32[1,1,7]{2,1,0:T(1,128)} %a_cols_ref.1, s32[2,1,7]{2,1,0:T(1,128)} %b_rows_ref.1, f32[896,128]{1,0:T(8,128)} %bitcast.9, f32[1792,128]{1,0:T(8,128)} %bitcast.8), custom_call_target="tpu_custom_call" | custom-call | flops 5637144576 | bytes 4194304 | tf_op jit(solution)/shard_map/gather_multiply_sum/pallas_call | solution.py:515
  86.1 1.4 %add_halves.1 = f32[16,2,128,128]{3,2,1,0:T(8,128)} custom-call(f32[16,2,128,128]{3,2,1,0:T(8,128)S(1)} %get-tuple-element.7.own_ref, f32[16,2,128,128]{3,2,1,0:T(8,128)S(1)} %get-tuple-element.8.arrived_ref), custom_call_target="tpu_custom_call" | custom-call | tf_op jit(solution)/shard_map/add_halves/pallas_call | solution.py:564
